TPU v7x, 32 devices: a whole 2x2x4 slice. The times are simulated.
32 devices in a mesh: dp: 8 (over z, x), tensor: 4 (over y, core).
Axes of the slice: x: 2, y: 2, z: 4, core: 2. Of those that a mesh axis runs over, the one named last changes fastest.
Arguments:
- tokens: bfloat16 [3072, 768], P('dp'), may hold values from -6 to 6
- segment_ids: int32 [3072], P('dp'), may hold values from -1 to 7, as said below
- cotangent: bfloat16 [3072, 768], P('dp'), may hold values from -6 to 6
- attn_input: bfloat16 [3, 768, 768], P(None, None, 'tensor'), may hold values from -3 to 3
- query_bias: float32 [768], P('tensor'), may hold values from -3 to 3
- value_bias: float32 [768], P('tensor'), may hold values from -3 to 3
- attn_output: bfloat16 [768, 768], P('tensor'), may hold values from -2 to 2
- output_bias: float32 [768], replicated, may hold values from -2 to 2
- gain_first: float32 [768], replicated, may hold values from 0.25 to 1.75
- shift_first: float32 [768], replicated, may hold values from -2 to 2
- hidden_weight: bfloat16 [768, 3072], P(None, 'tensor'), may hold values from -0.21875 to 0.21875
- hidden_bias: float32 [3072], P('tensor'), may hold values from -3 to 3
- down_weight: bfloat16 [3072, 768], P('tensor'), may hold values from -0.109375 to 0.109375
- down_bias: float32 [768], replicated, may hold values from -2 to 2
- gain_second: float32 [768], replicated, may hold values from 0.25 to 1.75
- shift_second: float32 [768], replicated, may hold values from -2 to 2
Outputs:
- block_out: bfloat16 [3072, 768], P('dp')
- input_grad: bfloat16 [3072, 768], P('dp')
- grad_attn_input: float32 [3, 768, 768], P(None, None, 'tensor')
- grad_query_bias: float32 [768], P('tensor')
- grad_value_bias: float32 [768], P('tensor')
- grad_attn_output: float32 [768, 768], P('tensor')
- grad_output_bias: float32 [768], replicated
- grad_gain_first: float32 [768], replicated
- grad_shift_first: float32 [768], replicated
- grad_hidden_weight: float32 [768, 3072], P(None, 'tensor')
- grad_hidden_bias: float32 [3072], P('tensor')
- grad_down_weight: float32 [3072, 768], P('tensor')
- grad_down_bias: float32 [768], replicated
- grad_gain_second: float32 [768], replicated
- grad_shift_second: float32 [768], replicated
Inputs may be any that keep to these rules, and one draw needn't show every extreme that they name: `segment_ids`: block g of 384 slots (the slots of one index of dp) begins with one sequence of id g, of 192 to 384 tokens; its remaining slots are padding with id -1. In every draw some block holds a sequence of 384 tokens.
All inputs are finite; a program needn't handle non-finite values.
Results may differ from a plain program's by a relative error of at most 0.011.
Values sent between devices are 32-bit elements; how exact they have to be, the bound alone decides.
A program may use at most 128 MiB of HBM per device.

v0:
```python
import jax
import jax.numpy as jnp
from jax import lax
from jax.sharding import PartitionSpec as P

HD = 64


EPSILON = 1e-05
TANH_SCALE = 0.7978845608028654
CUBIC = 0.044715


def norm_forward(values_in, norm_gain, norm_shift):
    row_mean = jnp.mean(values_in, axis=-1, keepdims=True)
    centered = values_in - row_mean
    inverse = lax.rsqrt(jnp.mean(centered * centered, axis=-1, keepdims=True) + EPSILON)
    normed = centered * inverse
    return (normed, inverse, normed * norm_gain + norm_shift)


def norm_backward(grad_out, normed, inverse, norm_gain):
    scaled = grad_out * norm_gain
    return inverse * (
        scaled
        - jnp.mean(scaled, axis=-1, keepdims=True)
        - normed * jnp.mean(scaled * normed, axis=-1, keepdims=True)
    )


def gelu_pair(pre_act):
    tangent = jnp.tanh(TANH_SCALE * (pre_act + CUBIC * pre_act * pre_act * pre_act))
    gelu_value = 0.5 * pre_act * (1.0 + tangent)
    gelu_slope = 0.5 * (1.0 + tangent) + 0.5 * pre_act * (1.0 - tangent * tangent) * TANH_SCALE * (
        1.0 + 3.0 * CUBIC * pre_act * pre_act
    )
    return (gelu_value, gelu_slope)


def contract_rows(left_mat, right_mat):
    return lax.dot_general(
        left_mat, right_mat, (((0,), (0,)), ((), ())), preferred_element_type=jnp.float32
    )


def contract_cols(left_mat, right_mat):
    return lax.dot_general(
        left_mat, right_mat, (((1,), (1,)), ((), ())), preferred_element_type=jnp.float32
    )


def allowed_mask(segments):
    position = jnp.arange(segments.shape[0])
    return (segments[:, None] == segments[None, :]) & (position[None, :] <= position[:, None])


def head_scores(queries, keys_bf, allowed):
    scaling = queries.shape[-1] ** (-0.5)
    scores = (
        jnp.einsum("qhd,khd->hqk", queries, keys_bf, preferred_element_type=jnp.float32) * scaling
    )
    return jnp.where(allowed[None], scores, -jnp.inf)


def attend(queries, keys_bf, values_bf, allowed):
    scores = head_scores(queries, keys_bf, allowed)
    top_score = jnp.max(scores, axis=-1, keepdims=True)
    log_sum = top_score + jnp.log(jnp.sum(jnp.exp(scores - top_score), axis=-1, keepdims=True))
    probs = jnp.exp(scores - log_sum).astype(jnp.bfloat16)
    mixed = jnp.einsum("hqk,khd->qhd", probs, values_bf, preferred_element_type=jnp.float32)
    return (mixed, log_sum)


def attend_back(queries, keys_bf, values_bf, allowed, log_sum, grad_mixed):
    probs_full = jnp.exp(head_scores(queries, keys_bf, allowed) - log_sum)
    probs_bf = probs_full.astype(jnp.bfloat16)
    grad_values = jnp.einsum(
        "hqk,qhd->khd", probs_bf, grad_mixed, preferred_element_type=jnp.float32
    )
    grad_probs = jnp.einsum(
        "qhd,khd->hqk", grad_mixed, values_bf, preferred_element_type=jnp.float32
    )
    scaling = queries.shape[-1] ** (-0.5)
    grad_scores = (
        probs_full
        * (grad_probs - jnp.sum(probs_full * grad_probs, axis=-1, keepdims=True))
        * scaling
    ).astype(jnp.bfloat16)
    grad_queries = jnp.einsum(
        "hqk,khd->qhd", grad_scores, keys_bf, preferred_element_type=jnp.float32
    )
    grad_keys = jnp.einsum("hqk,qhd->khd", grad_scores, queries, preferred_element_type=jnp.float32)
    return (grad_queries, grad_keys, grad_values)


def shards(
    tokens,
    segment_ids,
    cotangent,
    attn_input,
    query_bias,
    value_bias,
    attn_output,
    output_bias,
    gain_first,
    shift_first,
    hidden_weight,
    hidden_bias,
    down_weight,
    down_bias,
    gain_second,
    shift_second,
):
    row_count = tokens.shape[0]
    local_width = attn_input.shape[2]
    valid = (segment_ids >= 0)[:, None]
    cot_masked = jnp.where(valid, cotangent, jnp.zeros_like(cotangent))
    allowed = allowed_mask(segment_ids)
    resid_in = tokens.astype(jnp.float32)
    normed_one, inverse_one, pre_one = norm_forward(resid_in, gain_first, shift_first)
    hidden_one = pre_one.astype(jnp.bfloat16)
    projected = jnp.einsum(
        "rd,tdc->trc", hidden_one, attn_input, preferred_element_type=jnp.float32
    )
    queries = (projected[0] + query_bias).astype(jnp.bfloat16).reshape(row_count, -1, HD)
    keys_bf = projected[1].astype(jnp.bfloat16).reshape(row_count, -1, HD)
    values_bf = (projected[2] + value_bias).astype(jnp.bfloat16).reshape(row_count, -1, HD)
    mixed, log_sum = attend(queries, keys_bf, values_bf, allowed)
    attended = mixed.reshape(row_count, local_width).astype(jnp.bfloat16)
    attn_part = jnp.dot(attended, attn_output, preferred_element_type=jnp.float32)
    middle = resid_in + lax.psum(attn_part, "tensor") + output_bias
    normed_two, inverse_two, pre_two = norm_forward(middle, gain_second, shift_second)
    hidden_two = pre_two.astype(jnp.bfloat16)
    pre_act = jnp.dot(hidden_two, hidden_weight, preferred_element_type=jnp.float32) + hidden_bias
    gelu_value, gelu_slope = gelu_pair(pre_act)
    activation = gelu_value.astype(jnp.bfloat16)
    mlp_part = jnp.dot(activation, down_weight, preferred_element_type=jnp.float32)
    out_full = middle + lax.psum(mlp_part, "tensor") + down_bias
    block_out = jnp.where(valid, out_full, jnp.zeros_like(out_full)).astype(jnp.bfloat16)
    grad_top = cot_masked.astype(jnp.float32)
    grad_down_bias = jnp.sum(grad_top, axis=0)
    grad_down_weight = contract_rows(activation, cot_masked)
    grad_pre = contract_cols(cot_masked, down_weight) * gelu_slope
    grad_hidden_bias = jnp.sum(grad_pre, axis=0)
    grad_pre_bf = grad_pre.astype(jnp.bfloat16)
    grad_hidden_weight = contract_rows(hidden_two, grad_pre_bf)
    grad_two = lax.psum(contract_cols(grad_pre_bf, hidden_weight), "tensor")
    grad_gain_second = jnp.sum(grad_two * normed_two, axis=0)
    grad_shift_second = jnp.sum(grad_two, axis=0)
    grad_middle = grad_top + norm_backward(grad_two, normed_two, inverse_two, gain_second)
    grad_output_bias = jnp.sum(grad_middle, axis=0)
    grad_middle_bf = grad_middle.astype(jnp.bfloat16)
    grad_attn_output = contract_rows(attended, grad_middle_bf)
    grad_attended = (
        contract_cols(grad_middle_bf, attn_output).astype(jnp.bfloat16).reshape(row_count, -1, HD)
    )
    grad_queries, grad_keys, grad_values = attend_back(
        queries, keys_bf, values_bf, allowed, log_sum, grad_attended
    )
    grad_queries = grad_queries.reshape(row_count, local_width)
    grad_keys = grad_keys.reshape(row_count, local_width)
    grad_values = grad_values.reshape(row_count, local_width)
    grad_query_bias = jnp.sum(grad_queries, axis=0)
    grad_value_bias = jnp.sum(grad_values, axis=0)
    grad_stack = jnp.stack([grad_queries, grad_keys, grad_values]).astype(jnp.bfloat16)
    grad_attn_input = jnp.einsum(
        "rd,trc->tdc", hidden_one, grad_stack, preferred_element_type=jnp.float32
    )
    one_part = jnp.einsum("trc,tdc->rd", grad_stack, attn_input, preferred_element_type=jnp.float32)
    grad_one = lax.psum(one_part, "tensor")
    grad_gain_first = jnp.sum(grad_one * normed_one, axis=0)
    grad_shift_first = jnp.sum(grad_one, axis=0)
    input_grad = (
        grad_middle + norm_backward(grad_one, normed_one, inverse_one, gain_first)
    ).astype(jnp.bfloat16)
    (
        grad_attn_input,
        grad_query_bias,
        grad_value_bias,
        grad_attn_output,
        grad_output_bias,
        grad_gain_first,
        grad_shift_first,
        grad_hidden_weight,
        grad_hidden_bias,
        grad_down_weight,
        grad_down_bias,
        grad_gain_second,
        grad_shift_second,
    ) = lax.psum(
        (
            grad_attn_input,
            grad_query_bias,
            grad_value_bias,
            grad_attn_output,
            grad_output_bias,
            grad_gain_first,
            grad_shift_first,
            grad_hidden_weight,
            grad_hidden_bias,
            grad_down_weight,
            grad_down_bias,
            grad_gain_second,
            grad_shift_second,
        ),
        "dp",
    )
    return (
        block_out,
        input_grad,
        grad_attn_input,
        grad_query_bias,
        grad_value_bias,
        grad_attn_output,
        grad_output_bias,
        grad_gain_first,
        grad_shift_first,
        grad_hidden_weight,
        grad_hidden_bias,
        grad_down_weight,
        grad_down_bias,
        grad_gain_second,
        grad_shift_second,
    )


def solution(mesh):
    return jax.shard_map(
        shards,
        mesh=mesh,
        in_specs=(
            P("dp", None),
            P("dp"),
            P("dp", None),
            P(None, None, "tensor"),
            P("tensor"),
            P("tensor"),
            P("tensor", None),
            P(),
            P(),
            P(),
            P(None, "tensor"),
            P("tensor"),
            P("tensor", None),
            P(),
            P(),
            P(),
        ),
        out_specs=(
            P("dp", None),
            P("dp", None),
            P(None, None, "tensor"),
            P("tensor"),
            P("tensor"),
            P("tensor", None),
            P(),
            P(),
            P(),
            P(None, "tensor"),
            P("tensor"),
            P("tensor", None),
            P(),
            P(),
            P(),
        ),
        check_vma=False,
    )
```

profile of v0, /device:TPU:0, one launch (start us, length us, event | category | flops | bytes accessed | tf_op | source)
XLA Modules:
  0.0 433.0 jit_solution(2139666935853533905)
XLA Ops:
  7.3 1.3 convert_reduce_fusion
  8.6 1.4 fusion.24
  10.0 2.0 fusion.63
  15.1 1.4 fusion.77
  16.6 40.4 %all-reduce.8.cloned.1.call-done = f32[384,768]{1,0:T(8,128)} async-done(((f32[384,768]{1,0:T(8,128)}), f32[384,768]{1,0:T(8,128)}) %all-reduce.8.cloned.1.call-update) | async-done | bytes 1179664 | tf_op jit(solution)/shard_map/psum | solution.py:131
  56.9 1.5 fusion.68
  60.8 1.7 fusion.76
  63.3 1.7 fusion.51
  65.1 3.1 fusion.66
  68.2 34.7 %all-reduce.10.cloned.1.call-done = f32[384,768]{1,0:T(8,128)} async-done(((f32[384,768]{1,0:T(8,128)}), f32[384,768]{1,0:T(8,128)}) %all-reduce.10.cloned.1.call-update) | async-done | bytes 1179664 | tf_op jit(solution)/shard_map/psum | solution.py:147
  102.9 2.5 multiply_reduce_fusion.1
  105.5 2.0 fusion.67
  107.9 1.7 fusion.71
  109.6 1.8 fusion.55
  111.4 4.7 %fusion.34 = bf16[3,64,384]{2,1,0:T(8,128)(2,1)} fusion(f32[3,384,384]{1,2,0:T(8,128)} %fusion.55, f32[3,384,384]{1,2,0:T(8,128)} %copy-done.1, f32[3,384]{1,0:T(4,128)S(1)} %log_add_fusion, f32[384,3,64]{0,2,1:T(8,128)} %bitcast.52, f32[3,64]{1,0:T(4,128)} %copy-done.40), kind=kOutput, calls=%fused_computation.51 | convolution fusion | flops 59942400 | bytes 3986688 | tf_op jit(solution)/shard_map/hqk,qhd->khd/dot_general | solution.py:92
  116.1 5.4 %fusion.72 = (f32[3,64]{1,0:T(4,128)}, bf16[384,3,64]{0,2,1:T(8,128)(2,1)}) fusion(bf16[384,3,64]{0,2,1:T(8,128)(2,1)} %bitcast.56, f32[3,384,384]{1,2,0:T(8,128)} %fusion.55, f32[3,384,384]{1,2,0:T(8,128)} %copy-done.1, f32[3,384]{1,0:T(4,128)S(1)} %log_add_fusion), kind=kOutput, calls=%fused_computation.99 | convolution fusion | flops 59868480 | bytes 3839232 | tf_op jit(solution)/shard_map/hqk,khd->qhd/dot_general | solution.py:89
  121.5 3.1 convolution_bitcast_fusion.1
  125.2 3.8 fusion.65
  129.1 2.4 fusion.49
  131.5 1.1 fusion.46
  132.7 2.0 convolution_bitcast_fusion
  134.8 1.3 reduce_sum.188
  136.1 1.3 reduce_sum.186
  137.4 43.2 %all-reduce.14.cloned.1.call-done = (f32[384,768]{1,0:T(8,128)}, f32[384,768]{1,0:T(8,128)}) async-done(((f32[384,768]{1,0:T(8,128)}, f32[384,768]{1,0:T(8,128)}), (f32[384,768]{1,0:T(8,128)}, f32[384,768]{1,0:T(8,128)})) %all-reduce.14.cloned.1.call-update) | async-done | bytes 2359312 | tf_op jit(solution)/shard_map/psum | solution.py:138
  180.6 2.7 fusion.23
  183.3 40.2 %all-reduce = (f32[192]{0:T(256)}, f32[192]{0:T(256)}, f32[768]{0:T(1024)}, f32[768]{0:T(1024)}, f32[768]{0:T(1024)}, /*index=5*/f32[768]{0:T(1024)}, f32[768]{0:T(1024)}, f32[768]{0:T(1024)}, f32[768]{0:T(1024)}) all-reduce(f32[192]{0:T(256)} %reduce_sum.186, f32[192]{0:T(256)} %reduce_sum.188, ...), channel_id=1, replica_groups=mesh['dp'=8,'tensor'=4] {'dp'}, use_global_device_ids=true, to_apply=%region_17.18 | all-reduce | flops 5760 | bytes 46080 | tf_op jit(solution)/shard_map/psum | solution.py:190
  224.9 2.5 select_convert_fusion
  227.4 1.3 fusion.22
  228.6 190.2 %all-reduce.12.cloned.1.call-done = (f32[3,768,192]{1,2,0:T(8,128)}, f32[192,768]{1,0:T(8,128)}, f32[768,768]{1,0:T(8,128)}, f32[768,768]{1,0:T(8,128)}) async-done(((f32[3,768,192]{1,2,0:T(8,128)}, f32[192,768]{1,0:T(8,128)}, f32[768,768]{1,0:T(8,128)}, f32[768,768]{1,0:T(8,128)}), (f32[3,768,192]{1,2,0:T(8,128)}, f32[192,768]{1,0:T(8,128)}, f32[768,768]{1,0:T(8,128)}, ...) | async-done | bytes 7077904 | tf_op jit(solution)/shard_map/psum | solution.py:190
  418.8 2.9 copy.47
  422.6 1.4 copy.49
  425.1 1.4 copy.50
  (139 shorter events, 10.6 us)
Async XLA Ops:
  7.2 53.3 %copy-start = (bf16[768,768]{1,0:T(8,128)(2,1)S(1)}, bf16[768,768]{1,0:T(8,128)(2,1)}, u32[]{:S(2)}) copy-start(bf16[768,768]{1,0:T(8,128)(2,1)} %param.28) | copy-start | bytes 3538948
  7.2 2.8 copy-start.3
  7.2 2.8 copy-start.37
  7.2 2.8 copy-start.50
  7.2 49.7 %all-reduce.8.cloned.1.call-start = ((), (), s32[]{:S(2)}) async-start(), calls=%async_computation | async-start | bytes 2359296 | tf_op jit(solution)/shard_map/psum | solution.py:131
  8.6 3.4 copy-start.28
  10.0 2.0 copy-start.30
  15.1 41.9 %copy-start.44 = (f32[768]{0:T(1024)S(1)}, f32[768]{0:T(1024)}, u32[]{:S(2)}) copy-start(f32[768]{0:T(1024)} %param.23) | copy-start | bytes 9220
  16.5 86.4 %all-reduce.10.cloned.1.call-start = ((), (), s32[]{:S(2)}) async-start(), calls=%async_computation.1 | async-start | bytes 2359296 | tf_op jit(solution)/shard_map/psum | solution.py:147
  16.5 44.0 %copy-start.41 = (pred[384]{0:T(512)(128)(4,1)}, pred[384]{0:T(512)(128)(4,1)S(1)}, u32[]{:S(2)}) copy-start(pred[384]{0:T(512)(128)(4,1)S(1)} %broadcast_compare_fusion) | copy-start | bytes 1156
  59.7 43.2 %copy-start.26 = (f32[384]{0:T(512)}, f32[384]{0:T(512)S(1)}, u32[]{:S(2)}) copy-start(f32[384]{0:T(512)S(1)} %add_rsqrt_fusion) | copy-start | bytes 4612
  60.8 1.7 copy-start.54
  65.0 115.6 %all-reduce.14.cloned.1.call-start = ((), (), s32[]{:S(2)}) async-start(), calls=%async_computation.3 | async-start | bytes 4718592 | tf_op jit(solution)/shard_map/psum | solution.py:138
  102.9 2.6 copy-start.6
  102.9 2.6 copy-start.21
  102.9 2.6 copy-start.42
  105.5 2.0 copy-start.17
  105.5 2.4 copy-start.2
  107.9 1.7 copy-start.9
  124.6 4.4 %copy-start.27 = (f32[384]{0:T(512)S(1)}, f32[384]{0:T(512)}, u32[]{:S(2)}) copy-start(f32[384]{0:T(512)} %copy-done.26) | copy-start | bytes 4612
  124.6 294.2 %all-reduce.12.cloned.1.call-start = ((), (), s32[]{:S(2)}) async-start(), calls=%async_computation.2 | async-start | bytes 14155776 | tf_op jit(solution)/shard_map/psum | solution.py:190
  125.2 3.8 copy-start.11
  125.2 3.8 copy-start.46
  129.0 2.4 copy-start.15
  134.8 48.5 %copy-start.35 = (f32[768]{0:T(1024)S(1)}, f32[768]{0:T(1024)}, u32[]{:S(2)}) copy-start(f32[768]{0:T(1024)} %get-tuple-element.15) | copy-start | bytes 9220
  134.8 48.5 %copy-start.36 = (f32[768]{0:T(1024)S(1)}, f32[768]{0:T(1024)}, u32[]{:S(2)}) copy-start(f32[768]{0:T(1024)} %get-tuple-element.21) | copy-start | bytes 9220
  224.9 2.5 copy-start.5
  224.9 2.5 copy-start.7
  224.9 2.5 copy-start.39
  418.8 3.0 copy-start.23
  418.8 3.8 copy-start.13
  422.6 2.5 copy-start.12
  (27 other events, 30.5 us)
Sparse Core Ops, SparseCore 0:
  16.6 40.2 all-reduce.7
  65.2 37.7 all-reduce.9
  124.7 55.8 all-reduce.13
  186.0 232.7 all-reduce.11
where the time goes:
time: 434 us; the launch traced here: 433 us
  waiting for transfers between devices  309 us (71%)
  blocking collectives  40.2 us (9%)
  matrix products  38 us (9%)
  other arithmetic  17.2 us (4%)
  local copies, waits for them, and re-layouts  14.4 us (3%)
  between operations  14.3 us (3%)
    psum x1, waiting for transfers between devices, shards(): lax.psum((grad_attn_input, grad_query_bias, grad_value_bias, grad_attn_ou...  190 us
    psum x1, waiting for transfers between devices, shards(): out_full = middle + lax.psum(mlp_part, 'tensor') + down_bias  43.2 us
    psum x1, waiting for transfers between devices, shards(): middle = resid_in + lax.psum(attn_part, 'tensor') + output_bias  40.4 us
    psum x1, blocking collectives, shards(): lax.psum((grad_attn_input, grad_query_bias, grad_value_bias, grad_attn_ou...  40.2 us
    psum x1, waiting for transfers between devices, shards(): grad_two = lax.psum(contract_cols(grad_pre_bf, hidden_weight), 'tensor')  34.7 us
    unnamed x114, local copies, waits for them, and re-layouts  11.6 us
  transfers between devices with their start and end apart: 4, of which 4 were waited for; matrix products, arithmetic and copies ran while one was open for 5% of the time, Pallas kernels for 0%

commit v1 on v0

--- a/solution.py
+++ b/solution.py
@@ -1,9 +1,16 @@
 import jax
 import jax.numpy as jnp
 from jax import lax
+from jax.experimental import pallas as pl
+from jax.experimental.pallas import tpu as pltpu
 from jax.sharding import PartitionSpec as P
 
 HD = 64
+MESH = pl.DeviceIdType.MESH
+VM = pl.BlockSpec(memory_space=pltpu.VMEM)
+LIMIT = 60 * 1024 * 1024
+TPIECES = 4
+DPIECES = 4
 
 
 EPSILON = 1e-05
@@ -91,6 +98,312 @@
     )
     grad_keys = jnp.einsum("hqk,qhd->khd", grad_scores, queries, preferred_element_type=jnp.float32)
     return (grad_queries, grad_keys, grad_values)
+
+
+def push(src, dst, send_sem, recv_sem, device):
+    copy = pltpu.make_async_remote_copy(
+        src_ref=src,
+        dst_ref=dst,
+        send_sem=send_sem,
+        recv_sem=recv_sem,
+        device_id=device,
+        device_id_type=MESH,
+    )
+    copy.start()
+    return copy
+
+
+def tensor_scratch(count, rows, width):
+    piece = rows // 2 // TPIECES
+    buf = pltpu.VMEM((count * TPIECES, piece, width), jnp.float32)
+    sem = pltpu.SemaphoreType.DMA((count * TPIECES,))
+    return [buf] * 5 + [sem] * 6
+
+
+class TensorSum:
+    def __init__(self, parts, outs, scratch):
+        self.parts, self.outs = parts, outs
+        self.rx, self.mid, self.ry, self.fin, self.rb = scratch[:5]
+        self.sems = scratch[5:11]
+        dp = lax.axis_index("dp")
+        me = lax.axis_index("tensor")
+        low = me % 2
+        self.near = (dp, me + 1 - 2 * low)
+        self.far = (dp, me + 2 - 4 * (me // 2))
+        half = parts[0].shape[0] // 2
+        self.piece = half // TPIECES
+        self.mine, self.other = low * half, (1 - low) * half
+        self.units = [(a, k) for a in range(len(parts)) for k in range(TPIECES)]
+        self.copies = [[], [], []]
+
+    def peers(self):
+        return [self.near, self.far]
+
+    def window(self, base, k):
+        return pl.ds(pl.multiple_of(base + k * self.piece, 8), self.piece)
+
+    def send_halves(self):
+        for u, (a, k) in enumerate(self.units):
+            src = self.parts[a].at[self.window(self.other, k)]
+            self.copies[0].append(
+                push(src, self.rx.at[u], self.sems[0].at[u], self.sems[1].at[u], self.near)
+            )
+
+    def cross(self, u):
+        a, k = self.units[u]
+        self.copies[0][u].wait_recv()
+        self.mid[u] = self.parts[a][self.window(self.mine, k)] + self.rx[u]
+        self.copies[1].append(
+            push(self.mid.at[u], self.ry.at[u], self.sems[2].at[u], self.sems[3].at[u], self.far)
+        )
+
+    def finish(self, u):
+        a, k = self.units[u]
+        self.copies[1][u].wait_recv()
+        total = self.mid[u] + self.ry[u]
+        self.fin[u] = total
+        self.outs[a][self.window(self.mine, k)] = total
+        self.copies[2].append(
+            push(self.fin.at[u], self.rb.at[u], self.sems[4].at[u], self.sems[5].at[u], self.near)
+        )
+
+    def collect(self, u):
+        a, k = self.units[u]
+        self.copies[2][u].wait_recv()
+        self.outs[a][self.window(self.other, k)] = self.rb[u]
+
+    def drain(self):
+        for group in self.copies:
+            for copy in group:
+                copy.wait_send()
+
+
+def greet(peers):
+    barrier = pltpu.get_barrier_semaphore()
+    for peer in peers:
+        pl.semaphore_signal(barrier, inc=1, device_id=peer, device_id_type=MESH)
+    pl.semaphore_wait(barrier, len(peers))
+
+
+def tensor_kernel(count, *refs):
+    parts, outs, scratch = refs[:count], refs[count : 2 * count], refs[2 * count :]
+    job = TensorSum(parts, outs, scratch)
+    greet(job.peers())
+    job.send_halves()
+    for u in range(len(job.units)):
+        job.cross(u)
+    for u in range(len(job.units)):
+        job.finish(u)
+    for u in range(len(job.units)):
+        job.collect(u)
+    job.drain()
+
+
+def tensor_sum(parts, number):
+    rows, width = parts[0].shape
+    if lax.axis_size("tensor") != 4:
+        return lax.psum(parts, "tensor")
+    return pl.pallas_call(
+        lambda *refs: tensor_kernel(len(parts), *refs),
+        out_shape=[jax.ShapeDtypeStruct((rows, width), jnp.float32)] * len(parts),
+        in_specs=[VM] * len(parts),
+        out_specs=[VM] * len(parts),
+        scratch_shapes=tensor_scratch(len(parts), rows, width),
+        compiler_params=pltpu.CompilerParams(
+            collective_id=number, has_side_effects=True, vmem_limit_bytes=LIMIT
+        ),
+        name="tensor_sum",
+    )(*parts)
+
+
+def final_kernel(nt, nd, *refs):
+    refs = list(refs)
+    parts, mats, (normed, small) = refs[:nt], refs[nt : nt + nd], refs[nt + nd : nt + nd + 2]
+    refs = refs[nt + nd + 2 :]
+    part_outs, mat_outs, small_out = refs[:nt], refs[nt : nt + nd], refs[nt + nd]
+    refs = refs[nt + nd + 1 :]
+    job = TensorSum(parts, part_outs, refs[:11])
+    rx, own, rz, mid, ry, fin, re, rg = refs[11:19]
+    sx, qx, sz, qz, sy, qy, se, qe, sg, qg = refs[19:29]
+    slots, mine_small, ss, qs = refs[29:33]
+
+    dp = lax.axis_index("dp")
+    me = lax.axis_index("tensor")
+    column, line = dp % 2, dp // 2
+    inner = (line == 1) | (line == 2)
+    edge = (line == 0) | (line == 3)
+    across = (dp + 1 - 2 * column, me)
+    upper = line // 2
+    odd = line % 2
+    beside = ((line + 1 - 2 * odd) * 2 + column, me)
+    middle = ((1 - upper + 1) * 2 + column, me)
+    peers = [((dp + j) % 8, me) for j in range(1, 8)]
+    half = mats[0].shape[0] // 2
+    piece = half // DPIECES
+    units = [(a, k) for a in range(nd) for k in range(DPIECES)]
+    count = len(units)
+
+    def window(index, k):
+        return pl.ds(pl.multiple_of(index * half + k * piece, 8), piece)
+
+    def remote(src, dst, send, recv, device):
+        return pltpu.make_async_remote_copy(
+            src_ref=src,
+            dst_ref=dst,
+            send_sem=send,
+            recv_sem=recv,
+            device_id=device,
+            device_id_type=MESH,
+        )
+
+    def to_across(u):
+        a, k = units[u]
+        src = mats[a].at[window(1 - column, k)]
+        return remote(src, rx.at[u], sx.at[u], qx.at[u], across)
+
+    def to_middle_side(u):
+        return remote(own.at[u], rz.at[u], sz.at[u], qz.at[u], beside)
+
+    def between_middles(u):
+        return remote(mid.at[u], ry.at[u], sy.at[u], qy.at[u], middle)
+
+    def to_edge(u):
+        return remote(fin.at[u], re.at[u], se.at[u], qe.at[u], beside)
+
+    def give_back(u, src):
+        return remote(src.at[u], rg.at[u], sg.at[u], qg.at[u], across)
+
+    def stage_a(u):
+        a, k = units[u]
+        to_across(u).wait_recv()
+        own[u] = mats[a][window(column, k)] + rx[u]
+
+        @pl.when(edge)
+        def _():
+            to_middle_side(u).start()
+
+    def stage_b(u):
+        @pl.when(inner)
+        def _():
+            to_middle_side(u).wait_recv()
+            mid[u] = own[u] + rz[u]
+            between_middles(u).start()
+
+    def stage_c(u):
+        a, k = units[u]
+
+        @pl.when(inner)
+        def _():
+            between_middles(u).wait_recv()
+            total = mid[u] + ry[u]
+            fin[u] = total
+            to_edge(u).start()
+            give_back(u, fin).start()
+            mat_outs[a][window(column, k)] = total
+
+    def stage_d(u):
+        a, k = units[u]
+
+        @pl.when(edge)
+        def _():
+            to_edge(u).wait_recv()
+            give_back(u, re).start()
+            mat_outs[a][window(column, k)] = re[u]
+
+    def stage_e(u):
+        a, k = units[u]
+        give_back(u, fin).wait_recv()
+        mat_outs[a][window(1 - column, k)] = rg[u]
+
+    greet(peers + job.peers())
+    job.send_halves()
+    for u in range(count):
+        to_across(u).start()
+    for u in range(len(job.units)):
+        job.cross(u)
+    pending = list(range(len(job.units)))
+    stages = [stage_a, stage_b, stage_c, stage_d]
+    for step in range(count + len(stages) - 1):
+        for lag, stage in enumerate(stages):
+            if 0 <= step - lag < count:
+                stage(step - lag)
+        for _ in range(2):
+            if pending:
+                job.finish(pending.pop(0))
+    for u in pending:
+        job.finish(u)
+    for u in range(len(job.units)):
+        job.collect(u)
+
+    summed = part_outs[0][...]
+    row = lax.broadcasted_iota(jnp.int32, small.shape, 0)
+    gain = jnp.sum(summed * normed[...], axis=0, keepdims=True)
+    shift = jnp.sum(summed, axis=0, keepdims=True)
+    mine_small[...] = jnp.where(row == 0, gain, jnp.where(row == 1, shift, small[...]))
+    slots[dp] = mine_small[...]
+    notes = []
+    for j, peer in enumerate(peers):
+        notes.append(push(mine_small, slots.at[dp], ss.at[j], qs.at[j], peer))
+    for u in range(count):
+        stage_e(u)
+    for note in notes:
+        note.wait_recv()
+    total = slots[0]
+    for j in range(1, 8):
+        total = total + slots[j]
+    small_out[...] = total
+
+    job.drain()
+    for note in notes:
+        note.wait_send()
+    for u in range(count):
+        to_across(u).wait_send()
+        give_back(u, fin).wait_send()
+
+    @pl.when(edge)
+    def _():
+        for u in range(count):
+            to_middle_side(u).wait_send()
+
+    @pl.when(inner)
+    def _():
+        for u in range(count):
+            between_middles(u).wait_send()
+            to_edge(u).wait_send()
+
+
+def final_sums(parts, mats, normed, small, number):
+    nt, nd = len(parts), len(mats)
+    if lax.axis_size("tensor") != 4 or lax.axis_size("dp") != 8:
+        parts = tensor_sum(parts, number)
+        gain = jnp.sum(parts[0] * normed, axis=0)
+        small = small.at[0].set(gain).at[1].set(jnp.sum(parts[0], axis=0))
+        mats, small = lax.psum((mats, small), "dp")
+        return (parts, mats, small)
+    rows, width = mats[0].shape
+    count = nd * DPIECES
+    buf = pltpu.VMEM((count, rows // 2 // DPIECES, width), jnp.float32)
+    sem = pltpu.SemaphoreType.DMA((count,))
+    out = pl.pallas_call(
+        lambda *refs: final_kernel(nt, nd, *refs),
+        out_shape=[jax.ShapeDtypeStruct(p.shape, jnp.float32) for p in (*parts, *mats, small)],
+        in_specs=[VM] * (nt + nd + 2),
+        out_specs=[VM] * (nt + nd + 1),
+        scratch_shapes=tensor_scratch(nt, *parts[0].shape)
+        + [buf] * 8
+        + [sem] * 10
+        + [
+            pltpu.VMEM((8, *small.shape), jnp.float32),
+            pltpu.VMEM(small.shape, jnp.float32),
+            pltpu.SemaphoreType.DMA((7,)),
+            pltpu.SemaphoreType.DMA((7,)),
+        ],
+        compiler_params=pltpu.CompilerParams(
+            collective_id=number, has_side_effects=True, vmem_limit_bytes=LIMIT
+        ),
+        name="final_sums",
+    )(*parts, *mats, normed, small)
+    return (out[:nt], out[nt : nt + nd], out[nt + nd])
 
 
 def shards(
@@ -128,15 +441,13 @@
     mixed, log_sum = attend(queries, keys_bf, values_bf, allowed)
     attended = mixed.reshape(row_count, local_width).astype(jnp.bfloat16)
     attn_part = jnp.dot(attended, attn_output, preferred_element_type=jnp.float32)
-    middle = resid_in + lax.psum(attn_part, "tensor") + output_bias
+    middle = resid_in + tensor_sum([attn_part], 0)[0] + output_bias
     normed_two, inverse_two, pre_two = norm_forward(middle, gain_second, shift_second)
     hidden_two = pre_two.astype(jnp.bfloat16)
     pre_act = jnp.dot(hidden_two, hidden_weight, preferred_element_type=jnp.float32) + hidden_bias
     gelu_value, gelu_slope = gelu_pair(pre_act)
     activation = gelu_value.astype(jnp.bfloat16)
     mlp_part = jnp.dot(activation, down_weight, preferred_element_type=jnp.float32)
-    out_full = middle + lax.psum(mlp_part, "tensor") + down_bias
-    block_out = jnp.where(valid, out_full, jnp.zeros_like(out_full)).astype(jnp.bfloat16)
     grad_top = cot_masked.astype(jnp.float32)
     grad_down_bias = jnp.sum(grad_top, axis=0)
     grad_down_weight = contract_rows(activation, cot_masked)
@@ -144,13 +455,18 @@
     grad_hidden_bias = jnp.sum(grad_pre, axis=0)
     grad_pre_bf = grad_pre.astype(jnp.bfloat16)
     grad_hidden_weight = contract_rows(hidden_two, grad_pre_bf)
-    grad_two = lax.psum(contract_cols(grad_pre_bf, hidden_weight), "tensor")
+    two_part = contract_cols(grad_pre_bf, hidden_weight)
+    two_part, grad_hidden_weight, grad_down_weight = lax.optimization_barrier(
+        (two_part, grad_hidden_weight, grad_down_weight)
+    )
+    grad_hidden_weight, grad_down_weight = lax.psum((grad_hidden_weight, grad_down_weight), "dp")
+    grad_two = tensor_sum([two_part], 1)[0]
     grad_gain_second = jnp.sum(grad_two * normed_two, axis=0)
     grad_shift_second = jnp.sum(grad_two, axis=0)
     grad_middle = grad_top + norm_backward(grad_two, normed_two, inverse_two, gain_second)
     grad_output_bias = jnp.sum(grad_middle, axis=0)
     grad_middle_bf = grad_middle.astype(jnp.bfloat16)
-    grad_attn_output = contract_rows(attended, grad_middle_bf)
+    output_grad = contract_rows(grad_middle_bf, attended)
     grad_attended = (
         contract_cols(grad_middle_bf, attn_output).astype(jnp.bfloat16).reshape(row_count, -1, HD)
     )
@@ -162,49 +478,53 @@
     grad_values = grad_values.reshape(row_count, local_width)
     grad_query_bias = jnp.sum(grad_queries, axis=0)
     grad_value_bias = jnp.sum(grad_values, axis=0)
-    grad_stack = jnp.stack([grad_queries, grad_keys, grad_values]).astype(jnp.bfloat16)
-    grad_attn_input = jnp.einsum(
-        "rd,trc->tdc", hidden_one, grad_stack, preferred_element_type=jnp.float32
-    )
-    one_part = jnp.einsum("trc,tdc->rd", grad_stack, attn_input, preferred_element_type=jnp.float32)
-    grad_one = lax.psum(one_part, "tensor")
-    grad_gain_first = jnp.sum(grad_one * normed_one, axis=0)
-    grad_shift_first = jnp.sum(grad_one, axis=0)
+    grad_flat = jnp.concatenate([grad_queries, grad_keys, grad_values], axis=1).astype(jnp.bfloat16)
+    stack_grad = contract_rows(hidden_one, grad_flat)
+    attn_mat = jnp.concatenate([stack_grad, output_grad], axis=1)
+    attn_flat = jnp.concatenate([attn_input[0], attn_input[1], attn_input[2]], axis=1)
+    one_part = contract_cols(grad_flat, attn_flat)
+    width = tokens.shape[1]
+    zeros = jnp.zeros((2 * width,), jnp.float32)
+    pieces = [
+        zeros,
+        grad_output_bias,
+        grad_hidden_bias,
+        grad_down_bias,
+        grad_gain_second,
+        grad_shift_second,
+        grad_query_bias,
+        grad_value_bias,
+    ]
+    flat = jnp.concatenate(pieces)
+    rows = -(-flat.shape[0] // (8 * width)) * 8
+    small = jnp.pad(flat, (0, rows * width - flat.shape[0])).reshape(rows, width)
+    (grad_one, mlp_sum), (attn_mat,), small = final_sums(
+        [one_part, mlp_part], [attn_mat], normed_one, small, 2
+    )
     input_grad = (
         grad_middle + norm_backward(grad_one, normed_one, inverse_one, gain_first)
     ).astype(jnp.bfloat16)
+    out_full = middle + mlp_sum + down_bias
+    block_out = jnp.where(valid, out_full, jnp.zeros_like(out_full)).astype(jnp.bfloat16)
+    grad_attn_input = jnp.stack(
+        [attn_mat[:, m * local_width : (m + 1) * local_width] for m in range(3)]
+    )
+    grad_attn_output = attn_mat[:, 3 * local_width :].T
+    flat = small.reshape(-1)
+    grad_gain_first, grad_shift_first = flat[:width], flat[width : 2 * width]
+    values, start = [], 2 * width
+    for item in pieces[1:]:
+        values.append(flat[start : start + item.shape[0]])
+        start += item.shape[0]
     (
-        grad_attn_input,
-        grad_query_bias,
-        grad_value_bias,
-        grad_attn_output,
         grad_output_bias,
-        grad_gain_first,
-        grad_shift_first,
-        grad_hidden_weight,
         grad_hidden_bias,
-        grad_down_weight,
         grad_down_bias,
         grad_gain_second,
         grad_shift_second,
-    ) = lax.psum(
-        (
-            grad_attn_input,
-            grad_query_bias,
-            grad_value_bias,
-            grad_attn_output,
-            grad_output_bias,
-            grad_gain_first,
-            grad_shift_first,
-            grad_hidden_weight,
-            grad_hidden_bias,
-            grad_down_weight,
-            grad_down_bias,
-            grad_gain_second,
-            grad_shift_second,
-        ),
-        "dp",
-    )
+        grad_query_bias,
+        grad_value_bias,
+    ) = values
     return (
         block_out,
         input_grad,

time: 434 us -> 261 us (0.60)
  waiting for transfers between devices: 309 us -> 14.4 us
  Pallas kernels: 0 us -> 145 us
  blocking collectives: 40.2 us -> 0 us
  local copies, waits for them, and re-layouts: 14.4 us -> 31.4 us
  matrix products: 38 us -> 33.4 us
    psum x4 -> x1, waiting for transfers between devices: 308 us -> 14.3 us  [shards(): lax.psum((grad_hidden_weight, grad_down_weight), 'dp')]
    pallas_call x0 -> x3, Pallas kernels: none -> 145 us  [the longest x1 103 us: final_sums(): pl.pallas_call(lambda *refs: final_kernel(nt, nd, *refs), out_shape=[jax....]
    psum x1 -> x0, blocking collectives: 40.2 us -> none  [shards(): lax.psum((grad_attn_input, grad_query_bias, grad_value_bias, grad_attn_ou...]
    dot_general x2 -> x0, matrix products: 5.11 us -> none  [the longest x1 3.07 us: shards(): jnp.einsum('trc,tdc->rd', grad_stack, attn_input, preferred_element_type=...]
    unnamed x114 -> x100, local copies, waits for them, and re-layouts: 11.6 us -> 14 us
  transfers between devices with their start and end apart: 4 -> 1, of which waited for: 4 -> 1; matrix products, arithmetic and copies ran while one was open for 5% -> 22% of each run, Pallas kernels for 0% -> 48%
where the time goes in v1:
time: 261 us; the launch traced here: 260 us
  Pallas kernels  145 us (56%)
  matrix products  33.4 us (13%)
  local copies, waits for them, and re-layouts  31.4 us (12%)
  other arithmetic  21 us (8%)
  between operations  14.5 us (6%)
  waiting for transfers between devices  14.4 us (6%)
    pallas_call x1, Pallas kernels, final_sums(): pl.pallas_call(lambda *refs: final_kernel(nt, nd, *refs), out_shape=[jax....  103 us
    pallas_call x2, Pallas kernels, tensor_sum(): pl.pallas_call(lambda *refs: tensor_kernel(len(parts), *refs), out_shape=...  42 us
    psum x1, waiting for transfers between devices, shards(): lax.psum((grad_hidden_weight, grad_down_weight), 'dp')  14.3 us
    unnamed x100, local copies, waits for them, and re-layouts  14 us
    dot_general x4, matrix products, contract_rows(): lax.dot_general(left_mat, right_mat, (((0,), (0,)), ((), ())), preferred_...  6.09 us
    dot_general x4, matrix products, contract_cols(): lax.dot_general(left_mat, right_mat, (((1,), (1,)), ((), ())), preferred_...  5.63 us
    dot_general x1, matrix products, attend_back(): jnp.einsum('hqk,khd->qhd', grad_scores, keys_bf, preferred_element_type=j...  5.41 us
  transfers between devices with their start and end apart: 1, of which 1 were waited for; matrix products, arithmetic and copies ran while one was open for 22% of the time, Pallas kernels for 48%

profile of v1, /device:TPU:0, one launch (start us, length us, event | category | flops | bytes accessed | tf_op | source)
XLA Modules:
  0.0 259.8 jit_solution(16451260991479821841)
XLA Ops:
  10.2 1.4 fusion.12
  11.6 2.0 fusion.49
  16.5 1.4 fusion.72.refs_0_
  17.9 21.4 %tensor_sum.2 = f32[384,768]{1,0:T(8,128)} custom-call(f32[384,768]{1,0:T(8,128)} %fusion.72.refs_0_), custom_call_target="tpu_custom_call" | custom-call | tf_op jit(solution)/shard_map/tensor_sum/pallas_call | solution.py:206
  39.3 2.7 %fusion.62 = (f32[384]{0:T(512)S(1)}, f32[384,768]{1,0:T(8,128)S(1)}, f32[384,768]{1,0:T(8,128)}) fusion(f32[768]{0:T(1024)S(1)} %copy-done.36, f32[384,768]{1,0:T(8,128)} %tensor_sum.2, bf16[384,768]{1,0:T(8,128)(2,1)S(1)} %copy-done.3, f32[384]{0:T(512)S(1)} %add_rsqrt_fusion.1, f32[384]{0:T(512)S(1)} %broadcast_multiply_fusion.5), kind=kLoop, calls=%fused_computation.107 | loop fusion | flops 1769088 | bytes 4136448 | tf_op jit(solution)/shard_map/reduce_sum | solution.py:22
  44.4 2.4 fusion.58
  46.7 1.7 fusion.71
  48.5 1.7 fusion.44.refs_0_
  50.1 2.4 fusion.42
  52.5 20.5 %tensor_sum.3 = f32[384,768]{1,0:T(8,128)} custom-call(f32[384,768]{1,0:T(8,128)} %fusion.44.refs_0_), custom_call_target="tpu_custom_call" | custom-call | tf_op jit(solution)/shard_map/tensor_sum/pallas_call | solution.py:206
  73.1 2.5 multiply_reduce_fusion.2
  75.7 2.0 fusion.61
  78.1 1.7 fusion.65
  81.2 2.8 %fusion.50 = f32[3,384,384]{1,2,0:T(8,128)} fusion(bf16[384,3,64]{0,2,1:T(8,128)(2,1)} %bitcast.56, f32[384,3,64]{0,2,1:T(8,128)} %bitcast.52, f32[3,64]{1,0:T(4,128)S(1)} %copy-done.28), kind=kOutput, calls=%fused_computation.80 | convolution fusion | flops 56770560 | bytes 2212608 | tf_op jit(solution)/shard_map/qhd,khd->hqk/dot_general | solution.py:87
  84.0 5.4 %fusion.66 = (f32[3,64]{1,0:T(4,128)}, bf16[384,3,64]{0,2,1:T(8,128)(2,1)}) fusion(bf16[384,3,64]{0,2,1:T(8,128)(2,1)} %bitcast.63, f32[3,384,384]{1,2,0:T(8,128)} %fusion.50, f32[3,384,384]{1,2,0:T(8,128)} %copy-done.1, f32[3,384]{1,0:T(4,128)S(1)} %log_add_fusion), kind=kOutput, calls=%fused_computation.110 | convolution fusion | flops 59868480 | bytes 3839232 | tf_op jit(solution)/shard_map/hqk,khd->qhd/dot_general | solution.py:96
  91.3 1.5 concatenate.16
  92.8 1.4 pad.4
  95.5 4.8 %fusion.22 = bf16[3,64,384]{2,1,0:T(8,128)(2,1)} fusion(f32[3,384,384]{1,2,0:T(8,128)} %fusion.50, f32[3,384,384]{1,2,0:T(8,128)} %copy-done.1, f32[3,384]{1,0:T(4,128)S(1)} %log_add_fusion, f32[384,3,64]{0,2,1:T(8,128)} %bitcast.58, f32[3,64]{1,0:T(4,128)} %copy-done.32), kind=kOutput, calls=%fused_computation.42 | convolution fusion | flops 59942400 | bytes 3986688 | tf_op jit(solution)/shard_map/hqk,qhd->khd/dot_general | solution.py:99
  101.6 1.9 fusion.26.refs_0_
  105.4 1.7 pad_maximum_fusion.refs_2_
  107.2 1.9 fusion.57.refs_1_
  109.1 103.1 %final_sums.1 = (f32[384,768]{1,0:T(8,128)}, f32[384,768]{1,0:T(8,128)}, f32[768,768]{1,0:T(8,128)}, f32[8,768]{1,0:T(8,128)}) custom-call(f32[384,768]{1,0:T(8,128)} %fusion.26.refs_0_, f32[384,768]{1,0:T(8,128)} %fusion.57.refs_1_, f32[768,768]{1,0:T(8,128)} %pad_maximum_fusion.refs_2_, f32[384,768]{1,0:T(8,128)} %get-tuple-element.73.refs_3_, ...), custom_call_target="tpu_custom_call" | custom-call | tf_op jit(solution)/shard_map/final_sums/pallas_call | solution.py:387
  213.5 4.1 %slice_bitcast_fusion = (f32[192,768]{0,1:T(8,128)}, f32[1,768,192]{2,1,0:T(8,128)}, f32[1,768,192]{2,1,0:T(8,128)}, f32[1,768,192]{2,1,0:T(8,128)}) fusion(f32[768,768]{1,0:T(8,128)} %get-tuple-element.25), kind=kLoop, calls=%fused_computation.57 | loop fusion | bytes 4718592 | tf_op jit(solution)/shard_map/transpose | solution.py:512
  217.6 2.2 copy.38
  219.8 3.2 %pad_maximum_fusion.1 = f32[3,768,192]{2,1,0:T(8,128)} fusion(f32[1,768,192]{2,1,0:T(8,128)} %get-tuple-element.64, f32[1,768,192]{2,1,0:T(8,128)} %get-tuple-element.65, f32[1,768,192]{2,1,0:T(8,128)} %get-tuple-element.66), kind=kLoop, calls=%fused_computation.2 | loop fusion | flops 884736 | bytes 3538944 | tf_op jit(solution)/shard_map/stack | solution.py:509
  223.0 2.9 %copy.37 = f32[3,768,192]{1,2,0:T(8,128)} copy(f32[3,768,192]{2,1,0:T(8,128)} %pad_maximum_fusion.1) | data formatting | bytes 3538944
  225.9 1.7 slice_reduce_fusion
  227.6 1.9 multiply_reduce_fusion.5
  229.5 1.4 fusion.67
  233.8 14.3 %all-reduce.4.cloned.1.call-done = (f32[768,768]{1,0:T(8,128)}, f32[768,768]{1,0:T(8,128)}) async-done(((f32[768,768]{1,0:T(8,128)}, f32[768,768]{1,0:T(8,128)}), (f32[768,768]{1,0:T(8,128)}, f32[768,768]{1,0:T(8,128)})) %all-reduce.4.cloned.1.call-update) | async-done | bytes 4718608 | tf_op jit(solution)/shard_map/psum | solution.py:462
  248.2 3.4 %copy.47 = f32[768,768]{1,0:T(8,128)} copy(f32[768,768]{1,0:T(8,128)} %get-tuple-element.99) | data formatting | bytes 4718592
  251.5 1.4 copy.48
  (129 shorter events, 20.7 us)
Async XLA Ops:
  7.2 39.6 %copy-start = (bf16[768,768]{1,0:T(8,128)(2,1)S(1)}, bf16[768,768]{1,0:T(8,128)(2,1)}, u32[]{:S(2)}) copy-start(bf16[768,768]{1,0:T(8,128)(2,1)} %param.28) | copy-start | bytes 3538948
  7.2 4.4 %copy-start.3 = (bf16[384,768]{1,0:T(8,128)(2,1)S(1)}, bf16[384,768]{1,0:T(8,128)(2,1)}, u32[]{:S(2)}) copy-start(bf16[384,768]{1,0:T(8,128)(2,1)} %param.16) | copy-start | bytes 1769476
  7.2 4.4 %copy-start.30 = (f32[768]{0:T(1024)S(1)}, f32[768]{0:T(1024)}, u32[]{:S(2)}) copy-start(f32[768]{0:T(1024)} %param.24) | copy-start | bytes 9220
  7.2 4.4 %copy-start.42 = (f32[768]{0:T(1024)S(1)}, f32[768]{0:T(1024)}, u32[]{:S(2)}) copy-start(f32[768]{0:T(1024)} %param.25) | copy-start | bytes 9220
  7.2 240.9 %all-reduce.4.cloned.1.call-start = ((), (), s32[]{:S(2)}) async-start(), calls=%async_computation | async-start | bytes 9437184 | tf_op jit(solution)/shard_map/psum | solution.py:462
  8.1 38.7 %copy-start.33 = (pred[384]{0:T(512)(128)(4,1)}, pred[384]{0:T(512)(128)(4,1)S(1)}, u32[]{:S(2)}) copy-start(pred[384]{0:T(512)(128)(4,1)S(1)} %broadcast_compare_fusion) | copy-start | bytes 1156
  11.6 27.8 %copy-start.24 = (f32[384]{0:T(512)}, f32[384]{0:T(512)S(1)}, u32[]{:S(2)}) copy-start(f32[384]{0:T(512)S(1)} %add_rsqrt_fusion.1) | copy-start | bytes 4612
  13.6 1.4 copy-start.20
  16.2 1.6 copy-start.10
  17.9 21.5 %copy-start.36 = (f32[768]{0:T(1024)S(1)}, f32[768]{0:T(1024)}, u32[]{:S(2)}) copy-start(f32[768]{0:T(1024)} %param.23) | copy-start | bytes 9220
  42.0 1.3 copy-start.37
  42.0 1.3 copy-start.41
  43.3 29.8 %copy-start.26 = (f32[384]{0:T(512)}, f32[384]{0:T(512)S(1)}, u32[]{:S(2)}) copy-start(f32[384]{0:T(512)S(1)} %add_rsqrt_fusion) | copy-start | bytes 4612
  44.4 2.4 copy-start.46
  73.1 2.6 copy-start.6
  73.1 2.6 copy-start.19
  73.1 2.6 copy-start.23
  73.1 2.6 copy-start.34
  75.7 2.0 copy-start.14
  75.7 2.4 copy-start.2
  78.1 1.7 copy-start.12
  78.1 3.1 %copy-start.28 = (f32[3,64]{1,0:T(4,128)S(1)}, f32[3,64]{1,0:T(4,128)}, u32[]{:S(2)}) copy-start(f32[3,64]{1,0:T(4,128)} %copy-done.27) | copy-start | bytes 2308
  84.0 7.3 %copy-start.29 = (f32[768]{0:T(1024)S(1)}, f32[768]{0:T(1024)}, u32[]{:S(2)}) copy-start(f32[768]{0:T(1024)} %get-tuple-element.44) | copy-start | bytes 9220
  100.2 1.3 copy-start.44
  100.2 1.3 copy-start.45
  101.6 1.9 copy-start.11
  105.4 1.7 copy-start.47
  225.9 5.0 %copy-start.16 = (f32[384,768]{1,0:T(8,128)S(1)}, f32[384,768]{1,0:T(8,128)}, u32[]{:S(2)}) copy-start(f32[384,768]{1,0:T(8,128)} %get-tuple-element.23) | copy-start | bytes 3538948
  225.9 5.0 %copy-start.35 = (pred[384]{0:T(512)(128)(4,1)S(1)}, pred[384]{0:T(512)(128)(4,1)}, u32[]{:S(2)}) copy-start(pred[384]{0:T(512)(128)(4,1)} %copy-done.33) | copy-start | bytes 1156
  225.9 5.0 %copy-start.38 = (f32[768]{0:T(1024)S(1)}, f32[768]{0:T(1024)}, u32[]{:S(2)}) copy-start(f32[768]{0:T(1024)} %param.29) | copy-start | bytes 9220
  230.9 1.7 copy-start.7
  248.2 3.4 %copy-start.9 = (f32[768,768]{1,0:T(8,128)S(1)}, f32[768,768]{1,0:T(8,128)}, u32[]{:S(2)}) copy-start(f32[768,768]{1,0:T(8,128)} %get-tuple-element.101) | copy-start | bytes 7077892
  (17 other events, 17.4 us)
Sparse Core Ops, SparseCore 0:
  52.7 195.4 all-reduce.3

commit v2 on v0

--- a/solution.py
+++ b/solution.py
@@ -1,9 +1,16 @@
 import jax
 import jax.numpy as jnp
 from jax import lax
+from jax.experimental import pallas as pl
+from jax.experimental.pallas import tpu as pltpu
 from jax.sharding import PartitionSpec as P
 
 HD = 64
+MESH = pl.DeviceIdType.MESH
+VM = pl.BlockSpec(memory_space=pltpu.VMEM)
+LIMIT = 60 * 1024 * 1024
+TPIECES = 4
+DPIECES = 4
 
 
 EPSILON = 1e-05
@@ -93,7 +100,382 @@
     return (grad_queries, grad_keys, grad_values)
 
 
-def shards(
+def push(src, dst, send_sem, recv_sem, device):
+    copy = pltpu.make_async_remote_copy(
+        src_ref=src,
+        dst_ref=dst,
+        send_sem=send_sem,
+        recv_sem=recv_sem,
+        device_id=device,
+        device_id_type=MESH,
+    )
+    copy.start()
+    return copy
+
+
+def tensor_scratch(count, rows, width):
+    piece = rows // 2 // TPIECES
+    buf = pltpu.VMEM((count * TPIECES, piece, width), jnp.float32)
+    sem = pltpu.SemaphoreType.DMA((count * TPIECES,))
+    return [buf] * 5 + [sem] * 6
+
+
+class TensorSum:
+    def __init__(self, parts, outs, scratch):
+        self.parts, self.outs = parts, outs
+        self.rx, self.mid, self.ry, self.fin, self.rb = scratch[:5]
+        self.sems = scratch[5:11]
+        dp = lax.axis_index("dp")
+        me = lax.axis_index("tensor")
+        low = me % 2
+        self.near = (dp, me + 1 - 2 * low)
+        self.far = (dp, me + 2 - 4 * (me // 2))
+        half = parts[0].shape[0] // 2
+        self.piece = half // TPIECES
+        self.mine, self.other = low * half, (1 - low) * half
+        self.units = [(a, k) for a in range(len(parts)) for k in range(TPIECES)]
+        self.copies = [[], [], []]
+
+    def peers(self):
+        return [self.near, self.far]
+
+    def window(self, base, k):
+        return pl.ds(pl.multiple_of(base + k * self.piece, 8), self.piece)
+
+    def send_halves(self):
+        for u, (a, k) in enumerate(self.units):
+            src = self.parts[a].at[self.window(self.other, k)]
+            self.copies[0].append(
+                push(src, self.rx.at[u], self.sems[0].at[u], self.sems[1].at[u], self.near)
+            )
+
+    def cross(self, u):
+        a, k = self.units[u]
+        self.copies[0][u].wait_recv()
+        self.mid[u] = self.parts[a][self.window(self.mine, k)] + self.rx[u]
+        self.copies[1].append(
+            push(self.mid.at[u], self.ry.at[u], self.sems[2].at[u], self.sems[3].at[u], self.far)
+        )
+
+    def finish(self, u):
+        a, k = self.units[u]
+        self.copies[1][u].wait_recv()
+        total = self.mid[u] + self.ry[u]
+        self.fin[u] = total
+        self.outs[a][self.window(self.mine, k)] = total
+        self.copies[2].append(
+            push(self.fin.at[u], self.rb.at[u], self.sems[4].at[u], self.sems[5].at[u], self.near)
+        )
+
+    def collect(self, u):
+        a, k = self.units[u]
+        self.copies[2][u].wait_recv()
+        self.outs[a][self.window(self.other, k)] = self.rb[u]
+
+    def drain(self):
+        for group in self.copies:
+            for copy in group:
+                copy.wait_send()
+
+
+def greet(peers):
+    barrier = pltpu.get_barrier_semaphore()
+    for peer in peers:
+        pl.semaphore_signal(barrier, inc=1, device_id=peer, device_id_type=MESH)
+    pl.semaphore_wait(barrier, len(peers))
+
+
+def tensor_kernel(count, *refs):
+    parts, outs, scratch = refs[:count], refs[count : 2 * count], refs[2 * count :]
+    job = TensorSum(parts, outs, scratch)
+    greet(job.peers())
+    job.send_halves()
+    for u in range(len(job.units)):
+        job.cross(u)
+    for u in range(len(job.units)):
+        job.finish(u)
+    for u in range(len(job.units)):
+        job.collect(u)
+    job.drain()
+
+
+def tensor_sum(parts, number):
+    rows, width = parts[0].shape
+    if lax.axis_size("tensor") != 4:
+        return lax.psum(parts, "tensor")
+    return pl.pallas_call(
+        lambda *refs: tensor_kernel(len(parts), *refs),
+        out_shape=[jax.ShapeDtypeStruct((rows, width), jnp.float32)] * len(parts),
+        in_specs=[VM] * len(parts),
+        out_specs=[VM] * len(parts),
+        scratch_shapes=tensor_scratch(len(parts), rows, width),
+        compiler_params=pltpu.CompilerParams(
+            collective_id=number, has_side_effects=True, vmem_limit_bytes=LIMIT
+        ),
+        name="tensor_sum",
+    )(*parts)
+
+
+def dot(left, right, left_dim, right_dim):
+    return lax.dot_general(
+        left, right, (((left_dim,), (right_dim,)), ((), ())), preferred_element_type=jnp.float32
+    )
+
+
+def backward_kernel(heads, *refs):
+    (two_part, mlp_part, down_mat, hidden_mat, middle, tokens, cot, hidden_one, queries, keys, values) = refs[:11]
+    (attended, attn_output, attn_rows, seg_col, seg_row, vectors) = refs[11:17]
+    block_out, input_grad, down_out, hidden_out, attn_out, small_out = refs[17:23]
+    two_sum, mlp_sum, one_part, one_sum, attn_mat, grad_middle = refs[23:29]
+    job_two = TensorSum([two_part], [two_sum], refs[29:40])
+    job_mlp = TensorSum([mlp_part], [mlp_sum], refs[40:51])
+    job_one = TensorSum([one_part], [one_sum], refs[51:62])
+    rx, own, rz, ry, rg = refs[62:67]
+    sx, qx, sz, qz, sy, qy, sg, qg = refs[67:75]
+    slots, mine_small, ss, qs = refs[75:79]
+    mats, outs = [down_mat, hidden_mat, attn_mat], [down_out, hidden_out, attn_out]
+
+    dp = lax.axis_index("dp")
+    me = lax.axis_index("tensor")
+    column, line = dp % 2, dp // 2
+    inner = (line == 1) | (line == 2)
+    edge = (line == 0) | (line == 3)
+    across = (dp + 1 - 2 * column, me)
+    odd = line % 2
+    beside = ((line + 1 - 2 * odd) * 2 + column, me)
+    middle_peer = ((2 - line // 2) * 2 + column, me)
+    peers = [((dp + j) % 8, me) for j in range(1, 8)]
+    half = down_mat.shape[0] // 2
+    piece = half // DPIECES
+    units = [(m, k) for m in range(3) for k in range(DPIECES)]
+    count = len(units)
+
+    def window(index, k):
+        return pl.ds(pl.multiple_of(index * half + k * piece, 8), piece)
+
+    def remote(src, dst, send, recv, device):
+        return pltpu.make_async_remote_copy(
+            src_ref=src,
+            dst_ref=dst,
+            send_sem=send,
+            recv_sem=recv,
+            device_id=device,
+            device_id_type=MESH,
+        )
+
+    def to_across(u):
+        m, k = units[u]
+        src = mats[m].at[window(1 - column, k)]
+        return remote(src, rx.at[u], sx.at[u], qx.at[u], across)
+
+    def to_beside(u, src):
+        return remote(src, rz.at[u], sz.at[u], qz.at[u], beside)
+
+    def between_middles(u):
+        return remote(own.at[u], ry.at[u], sy.at[u], qy.at[u], middle_peer)
+
+    def give_back(u, src):
+        return remote(src, rg.at[u], sg.at[u], qg.at[u], across)
+
+    def done(u):
+        m, k = units[u]
+        return outs[m].at[window(column, k)]
+
+    def stage_a(u):
+        m, k = units[u]
+        to_across(u).wait_recv()
+        own[u] = mats[m][window(column, k)] + rx[u]
+
+        @pl.when(edge)
+        def _():
+            to_beside(u, own.at[u]).start()
+
+    def stage_b(u):
+        @pl.when(inner)
+        def _():
+            to_beside(u, own.at[u]).wait_recv()
+            own[u] = own[u] + rz[u]
+            between_middles(u).start()
+
+    def stage_c(u):
+        m, k = units[u]
+
+        @pl.when(inner)
+        def _():
+            between_middles(u).wait_recv()
+            outs[m][window(column, k)] = own[u] + ry[u]
+            to_beside(u, done(u)).start()
+            give_back(u, done(u)).start()
+
+    def stage_d(u):
+        m, k = units[u]
+
+        @pl.when(edge)
+        def _():
+            to_beside(u, own.at[u]).wait_recv()
+            give_back(u, rz.at[u]).start()
+            outs[m][window(column, k)] = rz[u]
+
+    def stage_e(u):
+        m, k = units[u]
+        give_back(u, own.at[u]).wait_recv()
+        outs[m][window(1 - column, k)] = rg[u]
+
+    stages = [stage_a, stage_b, stage_c, stage_d]
+
+    def step(at):
+        for lag, stage in enumerate(stages):
+            if 0 <= at - lag < count:
+                stage(at - lag)
+
+    def each(call, job):
+        for u in range(len(job.units)):
+            call(u)
+
+    greet(peers + job_two.peers())
+    job_two.send_halves()
+    job_mlp.send_halves()
+    for u in range(2 * DPIECES):
+        to_across(u).start()
+    each(job_two.cross, job_two)
+    each(job_mlp.cross, job_mlp)
+    each(job_two.finish, job_two)
+    each(job_two.collect, job_two)
+
+    gain_first, gain_second, down_bias = vectors[0:1, :], vectors[1:2, :], vectors[2:3, :]
+    normed_two, inverse_two, _ = norm_forward(middle[...], gain_second, 0.0)
+    grad_two = two_sum[...]
+    mine_small[...] = jnp.zeros_like(mine_small)
+    mine_small[0:2, :] = vectors[3:5, :]
+    mine_small[2:3, :] = jnp.sum(grad_two * normed_two, axis=0, keepdims=True)
+    mine_small[3:4, :] = jnp.sum(grad_two, axis=0, keepdims=True)
+    grad_mid = cot[...].astype(jnp.float32) + norm_backward(
+        grad_two, normed_two, inverse_two, gain_second
+    )
+    grad_middle[...] = grad_mid
+    mine_small[4:5, :] = jnp.sum(grad_mid, axis=0, keepdims=True)
+    mid_bf = grad_mid.astype(jnp.bfloat16)
+    row_count, local_width = attended.shape
+    attn_mat[3 * local_width :, :] = dot(attended[...], mid_bf, 0, 0)
+    step(0)
+    step(1)
+
+    row_at = lax.broadcasted_iota(jnp.int32, (row_count, row_count), 0)
+    col_at = lax.broadcasted_iota(jnp.int32, (row_count, row_count), 1)
+    allowed = (seg_col[...] == seg_row[...]) & (col_at <= row_at)
+    scaling = HD ** (-0.5)
+    normal = hidden_one[...]
+    for h in range(heads):
+        query, key, value = queries[h], keys[h], values[h]
+        scores = jnp.where(allowed, dot(query, key, 1, 1) * scaling, -jnp.inf)
+        top = jnp.max(scores, axis=-1, keepdims=True)
+        log_sum = top + jnp.log(jnp.sum(jnp.exp(scores - top), axis=-1, keepdims=True))
+        probs = jnp.exp(scores - log_sum)
+        grad_mixed = dot(mid_bf, attn_output[h * HD : (h + 1) * HD, :], 1, 1).astype(jnp.bfloat16)
+        grad_value = dot(probs.astype(jnp.bfloat16), grad_mixed, 0, 0)
+        grad_probs = dot(grad_mixed, value, 1, 1)
+        weighted = jnp.sum(probs * grad_probs, axis=-1, keepdims=True)
+        grad_scores = (probs * (grad_probs - weighted) * scaling).astype(jnp.bfloat16)
+        grad_query = dot(grad_scores, key, 1, 0)
+        grad_key = dot(grad_scores, query, 0, 0)
+        mine_small[8 + h : 9 + h, 0:HD] = jnp.sum(grad_query, axis=0, keepdims=True)
+        mine_small[8 + heads + h : 9 + heads + h, 0:HD] = jnp.sum(grad_value, axis=0, keepdims=True)
+        for m, item in enumerate((grad_query, grad_key, grad_value)):
+            item = item.astype(jnp.bfloat16)
+            start = m * local_width + h * HD
+            attn_mat[start : start + HD, :] = dot(item, normal, 0, 0)
+            term = dot(item, attn_rows[start : start + HD, :], 1, 0)
+            if h == 0 and m == 0:
+                one_part[...] = term
+            else:
+                one_part[...] += term
+        if h < heads - 1:
+            step(2 + h)
+    for u in range(2 * DPIECES, count):
+        to_across(u).start()
+    job_one.send_halves()
+    at = 1 + heads
+    step(at)
+    each(job_one.cross, job_one)
+    each(job_mlp.finish, job_mlp)
+    step(at + 1)
+    each(job_one.finish, job_one)
+    each(job_mlp.collect, job_mlp)
+    valid = seg_col[...] >= 0
+    full = middle[...] + mlp_sum[...] + down_bias
+    block_out[...] = jnp.where(valid, full, 0.0).astype(block_out.dtype)
+    step(at + 2)
+    each(job_one.collect, job_one)
+    normed_one, inverse_one, _ = norm_forward(tokens[...].astype(jnp.float32), gain_first, 0.0)
+    grad_one = one_sum[...]
+    mine_small[5:6, :] = jnp.sum(grad_one * normed_one, axis=0, keepdims=True)
+    mine_small[6:7, :] = jnp.sum(grad_one, axis=0, keepdims=True)
+    slots[dp] = mine_small[...]
+    notes = []
+    for j, peer in enumerate(peers):
+        notes.append(push(mine_small, slots.at[dp], ss.at[j], qs.at[j], peer))
+    step(at + 3)
+    back = norm_backward(grad_one, normed_one, inverse_one, gain_first)
+    input_grad[...] = (grad_middle[...] + back).astype(input_grad.dtype)
+    for i in range(at + 4, count + len(stages) - 1):
+        step(i)
+    for note in notes:
+        note.wait_recv()
+    total = slots[0]
+    for j in range(1, 8):
+        total = total + slots[j]
+    small_out[...] = total
+    for u in range(count):
+        stage_e(u)
+
+    for job in (job_two, job_mlp, job_one):
+        job.drain()
+    for note in notes:
+        note.wait_send()
+    for u in range(count):
+        to_across(u).wait_send()
+        to_beside(u, own.at[u]).wait_send()
+        give_back(u, own.at[u]).wait_send()
+
+    @pl.when(inner)
+    def _():
+        for u in range(count):
+            between_middles(u).wait_send()
+
+
+def backward_pass(operands, heads, number):
+    rows, width = operands[0].shape
+    square = jax.ShapeDtypeStruct((width, width), jnp.float32)
+    small = (16, width)
+    whole = pltpu.VMEM((rows, width), jnp.float32)
+    count = 3 * DPIECES
+    buf = pltpu.VMEM((count, width // 2 // DPIECES, width), jnp.float32)
+    sem = pltpu.SemaphoreType.DMA((count,))
+    tile = jax.ShapeDtypeStruct((rows, width), jnp.bfloat16)
+    return pl.pallas_call(
+        lambda *refs: backward_kernel(heads, *refs),
+        out_shape=[tile, tile, square, square, square, jax.ShapeDtypeStruct(small, jnp.float32)],
+        in_specs=[VM] * len(operands),
+        out_specs=[VM] * 6,
+        scratch_shapes=[whole] * 4
+        + [pltpu.VMEM((width, width), jnp.float32), whole]
+        + tensor_scratch(1, rows, width) * 3
+        + [buf] * 5
+        + [sem] * 8
+        + [
+            pltpu.VMEM((8, *small), jnp.float32),
+            pltpu.VMEM(small, jnp.float32),
+            pltpu.SemaphoreType.DMA((7,)),
+            pltpu.SemaphoreType.DMA((7,)),
+        ],
+        compiler_params=pltpu.CompilerParams(
+            collective_id=number, has_side_effects=True, vmem_limit_bytes=67043328
+        ),
+        name="backward_pass",
+    )(*operands)
+
+
+def plain_shards(
     tokens,
     segment_ids,
     cotangent,
@@ -224,6 +606,134 @@
     )
 
 
+def shards(
+    tokens,
+    segment_ids,
+    cotangent,
+    attn_input,
+    query_bias,
+    value_bias,
+    attn_output,
+    output_bias,
+    gain_first,
+    shift_first,
+    hidden_weight,
+    hidden_bias,
+    down_weight,
+    down_bias,
+    gain_second,
+    shift_second,
+):
+    if lax.axis_size("tensor") != 4 or lax.axis_size("dp") != 8:
+        return plain_shards(
+            tokens,
+            segment_ids,
+            cotangent,
+            attn_input,
+            query_bias,
+            value_bias,
+            attn_output,
+            output_bias,
+            gain_first,
+            shift_first,
+            hidden_weight,
+            hidden_bias,
+            down_weight,
+            down_bias,
+            gain_second,
+            shift_second,
+        )
+    row_count = tokens.shape[0]
+    local_width = attn_input.shape[2]
+    valid = (segment_ids >= 0)[:, None]
+    cot_masked = jnp.where(valid, cotangent, jnp.zeros_like(cotangent))
+    allowed = allowed_mask(segment_ids)
+    resid_in = tokens.astype(jnp.float32)
+    normed_one, inverse_one, pre_one = norm_forward(resid_in, gain_first, shift_first)
+    hidden_one = pre_one.astype(jnp.bfloat16)
+    projected = jnp.einsum(
+        "rd,tdc->trc", hidden_one, attn_input, preferred_element_type=jnp.float32
+    )
+    queries = (projected[0] + query_bias).astype(jnp.bfloat16).reshape(row_count, -1, HD)
+    keys_bf = projected[1].astype(jnp.bfloat16).reshape(row_count, -1, HD)
+    values_bf = (projected[2] + value_bias).astype(jnp.bfloat16).reshape(row_count, -1, HD)
+    mixed, log_sum = attend(queries, keys_bf, values_bf, allowed)
+    attended = mixed.reshape(row_count, local_width).astype(jnp.bfloat16)
+    attn_part = jnp.dot(attended, attn_output, preferred_element_type=jnp.float32)
+    middle = resid_in + tensor_sum([attn_part], 0)[0] + output_bias
+    normed_two, inverse_two, pre_two = norm_forward(middle, gain_second, shift_second)
+    hidden_two = pre_two.astype(jnp.bfloat16)
+    pre_act = jnp.dot(hidden_two, hidden_weight, preferred_element_type=jnp.float32) + hidden_bias
+    gelu_value, gelu_slope = gelu_pair(pre_act)
+    activation = gelu_value.astype(jnp.bfloat16)
+    mlp_part = jnp.dot(activation, down_weight, preferred_element_type=jnp.float32)
+    grad_top = cot_masked.astype(jnp.float32)
+    grad_down_bias = jnp.sum(grad_top, axis=0)
+    grad_down_weight = contract_rows(activation, cot_masked)
+    grad_pre = contract_cols(cot_masked, down_weight) * gelu_slope
+    grad_hidden_bias = jnp.sum(grad_pre, axis=0)
+    grad_pre_bf = grad_pre.astype(jnp.bfloat16)
+    grad_hidden_weight = contract_rows(hidden_two, grad_pre_bf)
+    two_part = contract_cols(grad_pre_bf, hidden_weight)
+    width = tokens.shape[1]
+    heads = local_width // HD
+    vectors = jnp.concatenate(
+        [gain_first, gain_second, down_bias, grad_hidden_bias, grad_down_bias]
+    ).reshape(5, width)
+    operands = (
+        two_part,
+        mlp_part,
+        grad_down_weight,
+        grad_hidden_weight,
+        middle,
+        tokens,
+        cot_masked,
+        hidden_one,
+        queries.transpose(1, 0, 2),
+        keys_bf.transpose(1, 0, 2),
+        values_bf.transpose(1, 0, 2),
+        attended,
+        attn_output,
+        attn_input.transpose(0, 2, 1).reshape(3 * local_width, width),
+        segment_ids[:, None],
+        segment_ids[None, :],
+        jnp.pad(vectors, ((0, 3), (0, 0))),
+    )
+    block_out, input_grad, grad_down_weight, grad_hidden_weight, attn_mat, small = backward_pass(
+        operands, heads, 2
+    )
+    grad_attn_input = attn_mat[: 3 * local_width].reshape(3, local_width, width).transpose(0, 2, 1)
+    grad_attn_output = attn_mat[3 * local_width :]
+    (
+        grad_hidden_bias,
+        grad_down_bias,
+        grad_gain_second,
+        grad_shift_second,
+        grad_output_bias,
+        grad_gain_first,
+        grad_shift_first,
+    ) = (small[r] for r in range(7))
+    grad_query_bias = small[8 : 8 + heads, :HD].reshape(local_width)
+    grad_value_bias = small[8 + heads : 8 + 2 * heads, :HD].reshape(local_width)
+    return (
+        block_out,
+        input_grad,
+        grad_attn_input,
+        grad_query_bias,
+        grad_value_bias,
+        grad_attn_output,
+        grad_output_bias,
+        grad_gain_first,
+        grad_shift_first,
+        grad_hidden_weight,
+        grad_hidden_bias,
+        grad_down_weight,
+        grad_down_bias,
+        grad_gain_second,
+        grad_shift_second,
+    )
+
+
 def solution(mesh):
     return jax.shard_map(
         shards,

time: 434 us -> 246 us (0.57)
  waiting for transfers between devices: 309 us -> 0 us
  Pallas kernels: 0 us -> 193 us
  blocking collectives: 40.2 us -> 0 us
  matrix products: 38 us -> 12.9 us
  local copies, waits for them, and re-layouts: 14.4 us -> 31.5 us
  between operations: 14.3 us -> 0.95 us
  other arithmetic: 17.2 us -> 6.16 us
    psum x4 -> x0, waiting for transfers between devices: 308 us -> none  [the longest x1 190 us: shards(): lax.psum((grad_attn_input, grad_query_bias, grad_value_bias, grad_attn_ou...]
    pallas_call x0 -> x2, Pallas kernels: none -> 193 us  [the longest x1 172 us: backward_pass(): pl.pallas_call(lambda *refs: backward_kernel(heads, *refs), out_shape=[ti...]
    psum x1 -> x0, blocking collectives: 40.2 us -> none  [shards(): lax.psum((grad_attn_input, grad_query_bias, grad_value_bias, grad_attn_ou...]
    dot_general x6 -> x0, matrix products: 18.7 us -> none  [the longest x1 5.4 us: attend_back(): jnp.einsum('hqk,khd->qhd', grad_scores, keys_bf, preferred_element_type=j...]
    slice x0 -> x4, local copies, waits for them, and re-layouts: none -> 7.24 us  [the longest x1 2.89 us: shards(): attn_mat[:3 * local_width].reshape(3, local_width, width).transpose(0, 2, 1)]
    reduce_sum x3 -> x1, other arithmetic: 7.2 us -> 0.43 us  [shards(): grad_down_bias = jnp.sum(grad_top, axis=0)]
    unnamed x114 -> x62, local copies, waits for them, and re-layouts: 11.6 us -> 14 us
  transfers between devices with their start and end apart: 4 -> 0, of which waited for: 4 -> 0; matrix products, arithmetic and copies ran while one was open for 5% -> 0% of each run, Pallas kernels for 0% -> 0%
where the time goes in v2:
time: 246 us; the launch traced here: 245 us
  Pallas kernels  193 us (78%)
  local copies, waits for them, and re-layouts  31.5 us (13%)
  matrix products  12.9 us (5%)
  other arithmetic  6.16 us (3%)
    pallas_call x1, Pallas kernels, backward_pass(): pl.pallas_call(lambda *refs: backward_kernel(heads, *refs), out_shape=[ti...  172 us
    pallas_call x1, Pallas kernels, tensor_sum(): pl.pallas_call(lambda *refs: tensor_kernel(len(parts), *refs), out_shape=...  21.4 us
    unnamed x62, local copies, waits for them, and re-layouts  14 us

profile of v2, /device:TPU:0, one launch (start us, length us, event | category | flops | bytes accessed | tf_op | source)
XLA Modules:
  0.0 245.0 jit_solution(8261585067464573687)
XLA Ops:
  0.7 0.8 broadcast_compare_fusion
  1.5 1.2 broadcast_in_dim.31.refs_15_
  4.3 1.2 convert_reduce_fusion
  5.5 1.4 fusion.2
  6.9 1.3 constant_dynamic-update-slice_fusion.4
  8.2 1.3 constant_dynamic-update-slice_fusion.3
  9.5 1.3 constant_dynamic-update-slice_fusion.2
  10.9 0.8 broadcast_in_dim.32.refs_14_
  14.3 0.9 copy.49
  16.4 0.8 copy.50.refs_11_
  17.2 1.4 fusion.29.refs_0_
  18.6 21.4 %tensor_sum.1 = f32[384,768]{1,0:T(8,128)} custom-call(f32[384,768]{1,0:T(8,128)} %fusion.29.refs_0_), custom_call_target="tpu_custom_call" | custom-call | tf_op jit(solution)/shard_map/tensor_sum/pallas_call | solution.py:206
  40.0 1.5 fusion.22
  41.9 1.4 copy-done.10
  44.5 1.1 fusion.27
  45.6 1.3 constant_dynamic-update-slice_fusion.1
  47.5 1.3 reshape.147
  48.8 1.4 pad.4.refs_16_
  50.2 1.7 fusion.16.refs_0_
  51.9 1.9 fusion.21.refs_1_
  53.7 2.3 fusion.20.refs_2_
  56.1 2.4 fusion.14.refs_3_
  58.4 172.0 %backward_pass.1 = (bf16[384,768]{1,0:T(8,128)(2,1)}, bf16[384,768]{1,0:T(8,128)(2,1)}, f32[768,768]{1,0:T(8,128)}, f32[768,768]{1,0:T(8,128)}, f32[768,768]{1,0:T(8,128)}, /*index=5*/f32[16,768]{1,0:T(8,128)}) custom-call(f32[384,768]{1,0:T(8,128)} %fusion.16.refs_0_, f32[384,768]{1,0:T(8,128)} %fusion.21.refs_1_, f32[768,768]{1,0:T(8,128)} %fusion.20.refs_2_, ...), custom_call_target="tpu_custom_call" | custom-call | tf_op jit(solution)/shard_map/backward_pass/pallas_call | solution.py:455
  230.4 0.8 fusion.25
  231.2 1.7 slice_reduce_fusion
  234.1 1.9 slice.49
  236.1 2.9 %slice.46 = f32[576,768]{1,0:T(8,128)} slice(f32[768,768]{1,0:T(8,128)} %get-tuple-element.23), slice={[0:576], [0:768]} | slice | bytes 3538944 | tf_op jit(solution)/shard_map/slice | solution.py:705
  238.9 0.8 copy.64
  239.8 0.8 copy.65
  241.0 1.4 copy.66
  242.4 1.1 copy-done.7
  243.6 1.4 copy.67
  (77 shorter events, 9.3 us)
Async XLA Ops:
  0.6 11.1 %copy-start.1 = (bf16[384,768]{1,0:T(8,128)(2,1)S(1)}, bf16[384,768]{1,0:T(8,128)(2,1)}, u32[]{:S(2)}) copy-start(bf16[384,768]{1,0:T(8,128)(2,1)} %refs_5_.1) | copy-start | bytes 1769476
  0.7 10.1 %copy-start.14 = (s32[384]{0:T(512)S(1)}, s32[384]{0:T(512)}, u32[]{:S(2)}) copy-start(s32[384]{0:T(512)} %param.17) | copy-start | bytes 4612
  0.7 7.5 %copy-start.16 = (f32[768]{0:T(1024)S(1)}, f32[768]{0:T(1024)}, u32[]{:S(2)}) copy-start(f32[768]{0:T(1024)} %param.30) | copy-start | bytes 9220
  0.7 6.2 %copy-start.15 = (f32[768]{0:T(1024)S(1)}, f32[768]{0:T(1024)}, u32[]{:S(2)}) copy-start(f32[768]{0:T(1024)} %param.24) | copy-start | bytes 9220
  0.7 8.8 %copy-start.21 = (f32[768]{0:T(1024)S(1)}, f32[768]{0:T(1024)}, u32[]{:S(2)}) copy-start(f32[768]{0:T(1024)} %param.29) | copy-start | bytes 9220
  0.7 11.0 %copy-start.17 = (f32[768]{0:T(1024)S(1)}, f32[768]{0:T(1024)}, u32[]{:S(2)}) copy-start(f32[768]{0:T(1024)} %param.25) | copy-start | bytes 9220
  0.7 11.0 %copy-start.13 = (bf16[384,768]{1,0:T(8,128)(2,1)S(1)}, bf16[384,768]{1,0:T(8,128)(2,1)}, u32[]{:S(2)}) copy-start(bf16[384,768]{1,0:T(8,128)(2,1)} %param.18) | copy-start | bytes 1769476
  11.7 1.2 copy-start.3
  12.2 1.4 copy-start.2
  12.2 41.6 %copy-start.6 = (bf16[384,768]{1,0:T(8,128)(2,1)}, bf16[384,768]{1,0:T(8,128)(2,1)S(1)}, u32[]{:S(2)}) copy-start(bf16[384,768]{1,0:T(8,128)(2,1)S(1)} %get-tuple-element.35.refs_6_) | copy-start | bytes 1769476
  14.0 1.7 copy-start.5
  14.3 1.7 copy-start.4
  16.0 1.3 copy-start.9
  18.6 21.4 %copy-start.18 = (f32[768]{0:T(1024)S(1)}, f32[768]{0:T(1024)}, u32[]{:S(2)}) copy-start(f32[768]{0:T(1024)} %param.23) | copy-start | bytes 9220
  41.5 14.5 %copy-start = (f32[384,768]{1,0:T(8,128)}, f32[384,768]{1,0:T(8,128)S(1)}, u32[]{:S(2)}) copy-start(f32[384,768]{1,0:T(8,128)S(1)} %get-tuple-element.37.refs_4_) | copy-start | bytes 3538948
  41.6 1.7 copy-start.10
  41.6 1.7 copy-start.19
  41.6 1.7 copy-start.24
  43.3 1.3 copy-start.22
  44.5 1.1 copy-start.25
  50.2 1.7 copy-start.23
  50.2 1.7 copy-start.26
  53.7 2.3 copy-start.20
  236.0 2.9 %copy-start.12 = (bf16[384,768]{1,0:T(8,128)(2,1)S(1)}, bf16[384,768]{1,0:T(8,128)(2,1)}, u32[]{:S(2)}) copy-start(bf16[384,768]{1,0:T(8,128)(2,1)} %get-tuple-element.64) | copy-start | bytes 1769476
  236.0 3.7 %copy-start.11 = (bf16[384,768]{1,0:T(8,128)(2,1)S(1)}, bf16[384,768]{1,0:T(8,128)(2,1)}, u32[]{:S(2)}) copy-start(bf16[384,768]{1,0:T(8,128)(2,1)} %get-tuple-element.65) | copy-start | bytes 1769476
  238.9 2.1 copy-start.8
  241.0 2.5 %copy-start.7 = (f32[768,768]{1,0:T(8,128)S(1)}, f32[768,768]{1,0:T(8,128)}, u32[]{:S(2)}) copy-start(f32[768,768]{1,0:T(8,128)} %get-tuple-element.75) | copy-start | bytes 7077892

commit v3 on v2

--- a/solution.py
+++ b/solution.py
@@ -233,6 +233,8 @@
     rx, own, rz, ry, rg = refs[62:67]
     sx, qx, sz, qz, sy, qy, sg, qg = refs[67:75]
     slots, mine_small, ss, qs = refs[75:79]
+    edge_in, sums, mid_in, side_in, mid_back = refs[79:84]
+    s_in, q_in, s_mid, q_mid, s_side, q_side, s_back, q_back, s_near, q_near, s_rest, q_rest = refs[84:96]
     mats, outs = [down_mat, hidden_mat, attn_mat], [down_out, hidden_out, attn_out]
 
     dp = lax.axis_index("dp")
@@ -245,13 +247,19 @@
     beside = ((line + 1 - 2 * odd) * 2 + column, me)
     middle_peer = ((2 - line // 2) * 2 + column, me)
     peers = [((dp + j) % 8, me) for j in range(1, 8)]
-    half = down_mat.shape[0] // 2
-    piece = half // DPIECES
-    units = [(m, k) for m in range(3) for k in range(DPIECES)]
+    full = down_mat.shape[0] // DPIECES
+    piece = full // 2
+    upper = line // 2
+    halves = DPIECES // 2
+    units = [(1, k) for k in range(DPIECES)] + [(2, k) for k in range(halves)]
+    line_units = [(0, k) for k in range(DPIECES)] + [(2, k) for k in range(halves, DPIECES)]
     count = len(units)
 
     def window(index, k):
-        return pl.ds(pl.multiple_of(index * half + k * piece, 8), piece)
+        return pl.ds(pl.multiple_of(k * full + index * piece, 8), piece)
+
+    def part(index):
+        return pl.ds(pl.multiple_of(index * piece, 8), piece)
 
     def remote(src, dst, send, recv, device):
         return pltpu.make_async_remote_copy(
@@ -321,12 +329,93 @@
         give_back(u, own.at[u]).wait_recv()
         outs[m][window(1 - column, k)] = rg[u]
 
-    stages = [stage_a, stage_b, stage_c, stage_d]
+    def line_in(u):
+        m, k = line_units[u]
+        src = mats[m].at[k * full : (k + 1) * full]
+        return remote(src, edge_in.at[u], s_in.at[u], q_in.at[u], beside)
+
+    def line_mid(u):
+        src = sums.at[u, part(1 - upper)]
+        return remote(src, mid_in.at[u], s_mid.at[u], q_mid.at[u], middle_peer)
+
+    def line_side(u):
+        src = sums.at[u, part(upper)]
+        return remote(src, side_in.at[u], s_side.at[u], q_side.at[u], across)
+
+    def line_done(u):
+        m, k = line_units[u]
+        return outs[m].at[window(upper, k)]
+
+    def line_back(u):
+        return remote(line_done(u), mid_back.at[u], s_back.at[u], q_back.at[u], middle_peer)
+
+    def line_near(u):
+        dst = edge_in.at[u, part(upper)]
+        return remote(line_done(u), dst, s_near.at[u], q_near.at[u], beside)
+
+    def line_rest(u):
+        dst = edge_in.at[u, part(1 - upper)]
+        return remote(mid_back.at[u], dst, s_rest.at[u], q_rest.at[u], beside)
+
+    def line_b(u):
+        m, k = line_units[u]
+
+        @pl.when(inner)
+        def _():
+            line_in(u).wait_recv()
+            sums[u] = mats[m][k * full : (k + 1) * full] + edge_in[u]
+            line_mid(u).start()
+
+    def line_c(u):
+        @pl.when(inner)
+        def _():
+            line_mid(u).wait_recv()
+            sums[u, part(upper)] = sums[u, part(upper)] + mid_in[u]
+            line_side(u).start()
+
+    def line_d(u):
+        m, k = line_units[u]
+
+        @pl.when(inner)
+        def _():
+            line_side(u).wait_recv()
+            outs[m][window(upper, k)] = sums[u, part(upper)] + side_in[u]
+            line_back(u).start()
+            line_near(u).start()
+
+    def line_e(u):
+        m, k = line_units[u]
+
+        @pl.when(inner)
+        def _():
+            line_back(u).wait_recv()
+            line_rest(u).start()
+            outs[m][window(1 - upper, k)] = mid_back[u]
+
+    def line_f(u):
+        m, k = line_units[u]
+
+        @pl.when(edge)
+        def _():
+            line_near(u).wait_recv()
+            line_rest(u).wait_recv()
+            outs[m][k * full : (k + 1) * full] = edge_in[u]
+
+    stages = [stage_a, stage_b, stage_c, stage_d, None]
+    line_stages = [line_b, line_c, line_d, line_e, line_f]
 
     def step(at):
-        for lag, stage in enumerate(stages):
+        for lag in range(len(stages)):
             if 0 <= at - lag < count:
-                stage(at - lag)
+                line_stages[lag](at - lag)
+                if stages[lag] is not None:
+                    stages[lag](at - lag)
+
+    def line_starts(first, last):
+        @pl.when(edge)
+        def _():
+            for u in range(first, last):
+                line_in(u).start()
 
     def each(call, job):
         for u in range(len(job.units)):
@@ -335,8 +424,9 @@
     greet(peers + job_two.peers())
     job_two.send_halves()
     job_mlp.send_halves()
-    for u in range(2 * DPIECES):
+    for u in range(DPIECES):
         to_across(u).start()
+    line_starts(0, DPIECES)
     each(job_two.cross, job_two)
     each(job_mlp.cross, job_mlp)
     each(job_two.finish, job_two)
@@ -358,7 +448,6 @@
     row_count, local_width = attended.shape
     attn_mat[3 * local_width :, :] = dot(attended[...], mid_bf, 0, 0)
     step(0)
-    step(1)
 
     row_at = lax.broadcasted_iota(jnp.int32, (row_count, row_count), 0)
     col_at = lax.broadcasted_iota(jnp.int32, (row_count, row_count), 1)
@@ -389,12 +478,11 @@
                 one_part[...] = term
             else:
                 one_part[...] += term
-        if h < heads - 1:
-            step(2 + h)
-    for u in range(2 * DPIECES, count):
+    for u in range(DPIECES, count):
         to_across(u).start()
+    line_starts(DPIECES, count)
     job_one.send_halves()
-    at = 1 + heads
+    at = 1
     step(at)
     each(job_one.cross, job_one)
     each(job_mlp.finish, job_mlp)
@@ -402,8 +490,8 @@
     each(job_one.finish, job_one)
     each(job_mlp.collect, job_mlp)
     valid = seg_col[...] >= 0
-    full = middle[...] + mlp_sum[...] + down_bias
-    block_out[...] = jnp.where(valid, full, 0.0).astype(block_out.dtype)
+    out_full = middle[...] + mlp_sum[...] + down_bias
+    block_out[...] = jnp.where(valid, out_full, 0.0).astype(block_out.dtype)
     step(at + 2)
     each(job_one.collect, job_one)
     normed_one, inverse_one, _ = norm_forward(tokens[...].astype(jnp.float32), gain_first, 0.0)
@@ -437,10 +525,20 @@
         to_beside(u, own.at[u]).wait_send()
         give_back(u, own.at[u]).wait_send()
 
+    @pl.when(edge)
+    def _():
+        for u in range(count):
+            line_in(u).wait_send()
+
     @pl.when(inner)
     def _():
         for u in range(count):
             between_middles(u).wait_send()
+            line_mid(u).wait_send()
+            line_side(u).wait_send()
+            line_back(u).wait_send()
+            line_near(u).wait_send()
+            line_rest(u).wait_send()
 
 
 def backward_pass(operands, heads, number):
@@ -448,8 +546,9 @@
     square = jax.ShapeDtypeStruct((width, width), jnp.float32)
     small = (16, width)
     whole = pltpu.VMEM((rows, width), jnp.float32)
-    count = 3 * DPIECES
+    count = 3 * DPIECES // 2
     buf = pltpu.VMEM((count, width // 2 // DPIECES, width), jnp.float32)
+    wide = pltpu.VMEM((count, width // DPIECES, width), jnp.float32)
     sem = pltpu.SemaphoreType.DMA((count,))
     tile = jax.ShapeDtypeStruct((rows, width), jnp.bfloat16)
     return pl.pallas_call(
@@ -467,7 +566,9 @@
             pltpu.VMEM(small, jnp.float32),
             pltpu.SemaphoreType.DMA((7,)),
             pltpu.SemaphoreType.DMA((7,)),
-        ],
+        ]
+        + [wide, wide, buf, buf, buf]
+        + [sem] * 12,
         compiler_params=pltpu.CompilerParams(
             collective_id=number, has_side_effects=True, vmem_limit_bytes=67043328
         ),

time: 246 us -> 301 us (1.22)
  Pallas kernels: 193 us -> 248 us
    pallas_call x1, Pallas kernels: 172 us -> 227 us  [backward_pass(): pl.pallas_call(lambda *refs: backward_kernel(heads, *refs), out_shape=[ti...]
where the time goes in v3:
time: 301 us; the launch traced here: 300 us
  Pallas kernels  248 us (82%)
  local copies, waits for them, and re-layouts  31.5 us (10%)
  matrix products  12.9 us (4%)
  other arithmetic  6.16 us (2%)
    pallas_call x1, Pallas kernels, backward_pass(): pl.pallas_call(lambda *refs: backward_kernel(heads, *refs), out_shape=[ti...  227 us
    pallas_call x1, Pallas kernels, tensor_sum(): pl.pallas_call(lambda *refs: tensor_kernel(len(parts), *refs), out_shape=...  21.4 us
    unnamed x62, local copies, waits for them, and re-layouts  14 us

profile of v3, /device:TPU:0, one launch (start us, length us, event | category | flops | bytes accessed | tf_op | source)
XLA Modules:
  0.0 299.9 jit_solution(14359604662265887206)
XLA Ops:
  0.7 0.8 broadcast_compare_fusion
  1.5 1.2 broadcast_in_dim.31.refs_15_
  4.3 1.2 convert_reduce_fusion
  5.5 1.4 fusion.2
  6.9 1.3 constant_dynamic-update-slice_fusion.4
  8.2 1.3 constant_dynamic-update-slice_fusion.3
  9.5 1.3 constant_dynamic-update-slice_fusion.2
  10.9 0.8 broadcast_in_dim.32.refs_14_
  14.3 0.9 copy.49
  16.4 0.8 copy.50.refs_11_
  17.2 1.4 fusion.29.refs_0_
  18.6 21.4 %tensor_sum.1 = f32[384,768]{1,0:T(8,128)} custom-call(f32[384,768]{1,0:T(8,128)} %fusion.29.refs_0_), custom_call_target="tpu_custom_call" | custom-call | tf_op jit(solution)/shard_map/tensor_sum/pallas_call | solution.py:206
  40.0 1.5 fusion.22
  41.9 1.4 copy-done.10
  44.5 1.1 fusion.27
  45.6 1.3 constant_dynamic-update-slice_fusion.1
  47.5 1.3 reshape.147
  48.8 1.4 pad.4.refs_16_
  50.2 1.7 fusion.16.refs_0_
  51.9 1.9 fusion.21.refs_1_
  53.7 2.3 fusion.20.refs_2_
  56.1 2.4 fusion.14.refs_3_
  58.4 227.0 %backward_pass.1 = (bf16[384,768]{1,0:T(8,128)(2,1)}, bf16[384,768]{1,0:T(8,128)(2,1)}, f32[768,768]{1,0:T(8,128)}, f32[768,768]{1,0:T(8,128)}, f32[768,768]{1,0:T(8,128)}, /*index=5*/f32[16,768]{1,0:T(8,128)}) custom-call(f32[384,768]{1,0:T(8,128)} %fusion.16.refs_0_, f32[384,768]{1,0:T(8,128)} %fusion.21.refs_1_, f32[768,768]{1,0:T(8,128)} %fusion.20.refs_2_, ...), custom_call_target="tpu_custom_call" | custom-call | tf_op jit(solution)/shard_map/backward_pass/pallas_call | solution.py:554
  285.4 0.8 fusion.25
  286.2 1.7 slice_reduce_fusion
  289.1 1.9 slice.49
  291.0 2.9 slice.46
  293.9 0.8 copy.64
  294.7 0.8 copy.65
  296.0 1.4 copy.66
  297.4 1.1 copy-done.7
  298.5 1.4 copy.67
  (77 shorter events, 9.3 us)
Async XLA Ops:
  0.6 11.1 %copy-start.1 = (bf16[384,768]{1,0:T(8,128)(2,1)S(1)}, bf16[384,768]{1,0:T(8,128)(2,1)}, u32[]{:S(2)}) copy-start(bf16[384,768]{1,0:T(8,128)(2,1)} %refs_5_.1) | copy-start | bytes 1769476
  0.7 10.1 %copy-start.14 = (s32[384]{0:T(512)S(1)}, s32[384]{0:T(512)}, u32[]{:S(2)}) copy-start(s32[384]{0:T(512)} %param.17) | copy-start | bytes 4612
  0.7 7.5 %copy-start.16 = (f32[768]{0:T(1024)S(1)}, f32[768]{0:T(1024)}, u32[]{:S(2)}) copy-start(f32[768]{0:T(1024)} %param.30) | copy-start | bytes 9220
  0.7 6.2 %copy-start.15 = (f32[768]{0:T(1024)S(1)}, f32[768]{0:T(1024)}, u32[]{:S(2)}) copy-start(f32[768]{0:T(1024)} %param.24) | copy-start | bytes 9220
  0.7 8.8 %copy-start.21 = (f32[768]{0:T(1024)S(1)}, f32[768]{0:T(1024)}, u32[]{:S(2)}) copy-start(f32[768]{0:T(1024)} %param.29) | copy-start | bytes 9220
  0.7 11.0 %copy-start.17 = (f32[768]{0:T(1024)S(1)}, f32[768]{0:T(1024)}, u32[]{:S(2)}) copy-start(f32[768]{0:T(1024)} %param.25) | copy-start | bytes 9220
  0.7 11.0 %copy-start.13 = (bf16[384,768]{1,0:T(8,128)(2,1)S(1)}, bf16[384,768]{1,0:T(8,128)(2,1)}, u32[]{:S(2)}) copy-start(bf16[384,768]{1,0:T(8,128)(2,1)} %param.18) | copy-start | bytes 1769476
  11.7 1.2 copy-start.3
  12.2 1.4 copy-start.2
  12.2 41.6 %copy-start.6 = (bf16[384,768]{1,0:T(8,128)(2,1)}, bf16[384,768]{1,0:T(8,128)(2,1)S(1)}, u32[]{:S(2)}) copy-start(bf16[384,768]{1,0:T(8,128)(2,1)S(1)} %get-tuple-element.35.refs_6_) | copy-start | bytes 1769476
  14.0 1.7 copy-start.5
  14.3 1.7 copy-start.4
  16.0 1.3 copy-start.9
  18.6 21.4 %copy-start.18 = (f32[768]{0:T(1024)S(1)}, f32[768]{0:T(1024)}, u32[]{:S(2)}) copy-start(f32[768]{0:T(1024)} %param.23) | copy-start | bytes 9220
  41.5 14.5 %copy-start = (f32[384,768]{1,0:T(8,128)}, f32[384,768]{1,0:T(8,128)S(1)}, u32[]{:S(2)}) copy-start(f32[384,768]{1,0:T(8,128)S(1)} %get-tuple-element.37.refs_4_) | copy-start | bytes 3538948
  41.6 1.7 copy-start.10
  41.6 1.7 copy-start.19
  41.6 1.7 copy-start.24
  43.3 1.3 copy-start.22
  44.5 1.1 copy-start.25
  50.2 1.7 copy-start.23
  50.2 1.7 copy-start.26
  53.7 2.3 copy-start.20
  291.0 2.9 copy-start.12
  291.0 3.7 %copy-start.11 = (bf16[384,768]{1,0:T(8,128)(2,1)S(1)}, bf16[384,768]{1,0:T(8,128)(2,1)}, u32[]{:S(2)}) copy-start(bf16[384,768]{1,0:T(8,128)(2,1)} %get-tuple-element.65) | copy-start | bytes 1769476
  293.9 2.1 copy-start.8
  296.0 2.5 copy-start.7
